TPU v7x, 128 devices: a whole 4x4x4 slice. The times are simulated.
128 devices in a mesh: seq: 8 (over z_lo, y), head: 16 (over x, z_hi, core).
Axes of the slice: x: 4, y: 4, z: 4 (z_hi: 2, z_lo: 2; z = z_hi * 2 + z_lo), core: 2. Of those that a mesh axis runs over, the one named last changes fastest.
Arguments:
- queries: bfloat16 [24576, 4096], P(('seq', 'head')), may hold values from -48 to 48
- keys: bfloat16 [24576, 2048], P(('seq', 'head')), may hold values from -4 to 4
- values: bfloat16 [24576, 2048], P(('seq', 'head')), may hold values from -6 to 6
- grad_out: bfloat16 [24576, 4096], P(('seq', 'head')), may hold values from -6 to 6
- doc_lengths: int32 [16], replicated, may hold values from 1 to 6144, 24576 in all
Outputs:
- grad_queries: bfloat16 [24576, 4096], P(('seq', 'head'))
- grad_keys: bfloat16 [24576, 2048], P(('seq', 'head'))
- grad_values: bfloat16 [24576, 2048], P(('seq', 'head'))
Inputs may be any that keep to these rules, and one draw needn't show every extreme that they name: `doc_lengths`: the lengths sum to 24576.
All inputs are finite; a program needn't handle non-finite values.
Results may differ from a plain program's by a relative error of at most 0.012.
Values may be sent and summed in bfloat16 or wider, within the bound.
A program may use at most 128 MiB of HBM per device.

v0:
```python
import jax
import jax.numpy as jnp
from jax import lax
from jax.sharding import PartitionSpec as P

HD = 128
WINDOW = 1024
QBLK = 512


def passed_along(shard, axis, by):
    count = lax.axis_size(axis)
    pairs = [(i, i + by) for i in range(count) if 0 <= i + by < count]
    return lax.ppermute(shard, axis, pairs)


def doc_index(doc_lengths, positions):
    doc_ends = jnp.cumsum(doc_lengths)
    return jnp.sum((positions[:, None] >= doc_ends[None, :]).astype(jnp.int32), axis=1)


def tile_grads(q_rows, out_rows, key_rows, value_rows, allowed):
    scaling = HD ** (-0.5)
    row_count = q_rows.shape[0]
    kv_count = key_rows.shape[1]
    per_group = q_rows.shape[1] // kv_count
    q_four = q_rows.reshape(row_count, kv_count, per_group, HD)
    out_four = out_rows.reshape(row_count, kv_count, per_group, HD)
    scores = (
        jnp.einsum("qagd,kad->agqk", q_four, key_rows, preferred_element_type=jnp.float32) * scaling
    )
    scores = jnp.where(allowed[None, None], scores, -jnp.inf)
    row_max = jnp.max(scores, axis=3, keepdims=True)
    exponent = jnp.exp(scores - row_max)
    weights = exponent / jnp.sum(exponent, axis=3, keepdims=True)
    weights_b = weights.astype(jnp.bfloat16)
    grad_values = jnp.einsum(
        "agqk,qagd->kad", weights_b, out_four, preferred_element_type=jnp.float32
    )
    grad_weights = jnp.einsum(
        "qagd,kad->agqk", out_four, value_rows, preferred_element_type=jnp.float32
    )
    row_dot = jnp.sum(weights * grad_weights, axis=3, keepdims=True)
    grad_scores = (weights * (grad_weights - row_dot) * scaling).astype(jnp.bfloat16)
    grad_query = jnp.einsum(
        "agqk,kad->qagd", grad_scores, key_rows, preferred_element_type=jnp.float32
    )
    grad_keys = jnp.einsum(
        "agqk,qagd->kad", grad_scores, q_four, preferred_element_type=jnp.float32
    )
    return (grad_query.reshape(row_count, kv_count * per_group, HD), grad_keys, grad_values)


def block_pass(count, q_all, out_all, key_src, value_src, src_offset, q_docs, k_docs, group_first):
    span = QBLK + WINDOW
    q_iota = jnp.arange(QBLK, dtype=jnp.int32)
    k_iota = jnp.arange(span, dtype=jnp.int32)

    def advance(totals, block):
        key_total, value_total = totals
        first_row = block * QBLK
        key_first = first_row - src_offset
        q_rows = lax.dynamic_slice_in_dim(q_all, first_row, QBLK, 0)
        out_rows = lax.dynamic_slice_in_dim(out_all, first_row, QBLK, 0)
        key_rows = lax.dynamic_slice_in_dim(key_src, key_first, span, 0)
        value_rows = lax.dynamic_slice_in_dim(value_src, key_first, span, 0)
        q_pos = group_first + first_row + q_iota
        k_pos = group_first + first_row - WINDOW + k_iota
        q_doc = lax.dynamic_slice_in_dim(q_docs, first_row, QBLK, 0)
        k_doc = lax.dynamic_slice_in_dim(k_docs, first_row, span, 0)
        allowed = (q_doc[:, None] == k_doc[None, :]) & (k_pos[None, :] <= q_pos[:, None])
        allowed = allowed & (q_pos[:, None] - k_pos[None, :] < WINDOW) & (k_pos[None, :] >= 0)
        grad_query, grad_keys, grad_values = tile_grads(
            q_rows, out_rows, key_rows, value_rows, allowed
        )
        key_total = lax.dynamic_update_slice_in_dim(
            key_total,
            lax.dynamic_slice_in_dim(key_total, key_first, span, 0) + grad_keys,
            key_first,
            0,
        )
        value_total = lax.dynamic_update_slice_in_dim(
            value_total,
            lax.dynamic_slice_in_dim(value_total, key_first, span, 0) + grad_values,
            key_first,
            0,
        )
        return ((key_total, value_total), grad_query)

    zeros_src = jnp.zeros(key_src.shape, jnp.float32)
    totals, grad_query = lax.scan(
        advance, (zeros_src, zeros_src), jnp.arange(count, dtype=jnp.int32)
    )
    return (totals[0], totals[1], grad_query.reshape((count * QBLK,) + q_all.shape[1:]))


def attend(queries, keys, values, grad_out, doc_lengths):
    group = queries.shape[0]
    group_first = lax.axis_index("seq") * group
    rims = jnp.stack([keys[group - WINDOW :], values[group - WINDOW :]])
    earlier = passed_along(rims, "seq", 1)
    key_ext = jnp.concatenate([earlier[0], keys], axis=0)
    value_ext = jnp.concatenate([earlier[1], values], axis=0)
    q_docs = doc_index(doc_lengths, group_first + jnp.arange(group, dtype=jnp.int32))
    k_docs = doc_index(
        doc_lengths, group_first - WINDOW + jnp.arange(group + WINDOW, dtype=jnp.int32)
    )
    blocks = group // QBLK
    key_total, value_total, grad_query = block_pass(
        blocks, queries, grad_out, key_ext, value_ext, 0, q_docs, k_docs, group_first
    )
    rim_keys = key_total[:WINDOW]
    rim_values = value_total[:WINDOW]
    own_keys = key_total[WINDOW:]
    own_values = value_total[WINDOW:]
    returned = passed_along(
        jnp.stack([rim_keys, rim_values]).astype(jnp.bfloat16), "seq", -1
    ).astype(jnp.float32)
    tail_keys = own_keys[group - WINDOW :] + returned[0]
    tail_values = own_values[group - WINDOW :] + returned[1]
    grad_keys = jnp.concatenate([own_keys[: group - WINDOW], tail_keys], axis=0).astype(
        jnp.bfloat16
    )
    grad_values = jnp.concatenate([own_values[: group - WINDOW], tail_values], axis=0).astype(
        jnp.bfloat16
    )
    return (grad_query.astype(jnp.bfloat16), grad_keys, grad_values)


def local(queries, keys, values, grad_out, doc_lengths):
    head_query, head_keys, head_values, head_out = (
        lax.all_to_all(queries, "head", split_axis=1, concat_axis=0, tiled=True),
        lax.all_to_all(keys, "head", split_axis=1, concat_axis=0, tiled=True),
        lax.all_to_all(values, "head", split_axis=1, concat_axis=0, tiled=True),
        lax.all_to_all(grad_out, "head", split_axis=1, concat_axis=0, tiled=True),
    )
    group = head_query.shape[0]
    grad_query, grad_keys, grad_values = attend(
        head_query.reshape(group, -1, HD),
        head_keys.reshape(group, -1, HD),
        head_values.reshape(group, -1, HD),
        head_out.reshape(group, -1, HD),
        doc_lengths,
    )
    return (
        lax.all_to_all(
            grad_query.reshape(group, -1), "head", split_axis=0, concat_axis=1, tiled=True
        ),
        lax.all_to_all(
            grad_keys.reshape(group, -1), "head", split_axis=0, concat_axis=1, tiled=True
        ),
        lax.all_to_all(
            grad_values.reshape(group, -1), "head", split_axis=0, concat_axis=1, tiled=True
        ),
    )


def solution(mesh):
    return jax.shard_map(
        local,
        mesh=mesh,
        in_specs=(
            P(("seq", "head"), None),
            P(("seq", "head"), None),
            P(("seq", "head"), None),
            P(("seq", "head"), None),
            P(),
        ),
        out_specs=(P(("seq", "head"), None), P(("seq", "head"), None), P(("seq", "head"), None)),
        check_vma=False,
    )
```

profile of v0, /device:TPU:7, one launch (start us, length us, event | category | flops | bytes accessed | tf_op | source)
XLA Modules:
  0.0 458.1 jit_solution(1640673268618918113)
XLA Ops:
  2.9 8.4 %all-to-all-start.2 = ((bf16[192,16,128]{2,0,1:T(8,128)(2,1)}), bf16[192,16,128]{2,0,1:T(8,128)(2,1)S(1)}, u32[]{:S(2)}, u32[]{:S(2)}) async-start(bf16[192,16,128]{2,0,1:T(8,128)(2,1)} %copy_bitcast_fusion.4), calls=%async_computation.2 | async-start | bytes 1572864 | tf_op jit(solution)/shard_map/all_to_all | solution.py:134
  12.4 11.3 %all-to-all-done.2 = bf16[192,16,128]{2,0,1:T(8,128)(2,1)S(1)} async-done(((bf16[192,16,128]{2,0,1:T(8,128)(2,1)}), bf16[192,16,128]{2,0,1:T(8,128)(2,1)S(1)}, u32[]{:S(2)}, u32[]{:S(2)}) %all-to-all-start.2) | async-done | bytes 786464 | tf_op jit(solution)/shard_map/all_to_all | solution.py:134
  23.7 6.3 %all-to-all-start.1 = ((bf16[192,16,128]{2,0,1:T(8,128)(2,1)}), bf16[192,16,128]{2,0,1:T(8,128)(2,1)S(1)}, u32[]{:S(2)}, u32[]{:S(2)}) async-start(bf16[192,16,128]{2,0,1:T(8,128)(2,1)} %copy_bitcast_fusion.5), calls=%async_computation.1 | async-start | bytes 1572864 | tf_op jit(solution)/shard_map/all_to_all | solution.py:133
  30.0 2.7 copy.120
  32.7 9.7 %all-to-all-done.1 = bf16[192,16,128]{2,0,1:T(8,128)(2,1)S(1)} async-done(((bf16[192,16,128]{2,0,1:T(8,128)(2,1)}), bf16[192,16,128]{2,0,1:T(8,128)(2,1)S(1)}, u32[]{:S(2)}, u32[]{:S(2)}) %all-to-all-start.1) | async-done | bytes 786464 | tf_op jit(solution)/shard_map/all_to_all | solution.py:133
  43.3 6.4 %all-to-all-start = ((bf16[192,16,256]{2,0,1:T(8,128)(2,1)}), bf16[192,16,256]{2,0,1:T(8,128)(2,1)S(1)}, u32[]{:S(2)}, u32[]{:S(2)}) async-start(bf16[192,16,256]{2,0,1:T(8,128)(2,1)} %bitcast.161), calls=%async_computation | async-start | bytes 3145728 | tf_op jit(solution)/shard_map/all_to_all | solution.py:132
  49.8 2.7 copy.119
  52.5 18.1 %all-to-all-done = bf16[192,16,256]{2,0,1:T(8,128)(2,1)S(1)} async-done(((bf16[192,16,256]{2,0,1:T(8,128)(2,1)}), bf16[192,16,256]{2,0,1:T(8,128)(2,1)S(1)}, u32[]{:S(2)}, u32[]{:S(2)}) %all-to-all-start) | async-done | bytes 1572896 | tf_op jit(solution)/shard_map/all_to_all | solution.py:132
  70.6 6.7 %all-to-all-start.3 = ((bf16[192,16,256]{2,0,1:T(8,128)(2,1)}), bf16[192,16,256]{2,0,1:T(8,128)(2,1)S(1)}, u32[]{:S(2)}, u32[]{:S(2)}) async-start(bf16[192,16,256]{2,0,1:T(8,128)(2,1)} %bitcast.160), calls=%async_computation.3 | async-start | bytes 3145728 | tf_op jit(solution)/shard_map/all_to_all | solution.py:135
  79.2 4.0 collective-permute-start
  83.7 9.9 %collective-permute-done = bf16[2,1024,1,128]{3,1,2,0:T(8,128)(2,1)} collective-permute-done((bf16[2,1024,1,128]{3,1,2,0:T(8,128)(2,1)}, bf16[2,1024,1,128]{3,1,2,0:T(8,128)(2,1)}, u32[]{:S(2)}, u32[]{:S(2)}) %collective-permute-start) | collective-permute-done | bytes 524320 | tf_op jit(solution)/shard_map/ppermute | solution.py:14
  94.7 2.8 pad_maximum_fusion
  99.3 10.2 %all-to-all-done.3 = bf16[192,16,256]{2,0,1:T(8,128)(2,1)S(1)} async-done(((bf16[192,16,256]{2,0,1:T(8,128)(2,1)}), bf16[192,16,256]{2,0,1:T(8,128)(2,1)S(1)}, u32[]{:S(2)}, u32[]{:S(2)}) %all-to-all-start.3) | async-done | bytes 1572896 | tf_op jit(solution)/shard_map/all_to_all | solution.py:135
  114.4 258.0 %while.17 = (s32[]{:T(128)}, f32[4096,1,128]{2,0,1:T(8,128)}, f32[4096,1,128]{2,0,1:T(8,128)}, bf16[6,512,2,128]{1,3,2,0:T(8,128)(2,1)}, s32[6]{0:T(128)S(1)}, /...) while((s32[]{:T(128)}, f32[4096,1,128]{2,0,1:T(8,128)}, ...), condition=%wide.region_7.8_spmd.clone, body=%wide.region_3.7_spmd.clone.sunk | while | flops 2060060672 | bytes 108224424 | solution.py:91
  118.7 2.4 fusion.76
  123.8 3.5 fusion.79
  134.0 3.2 fusion.81
  137.2 2.4 copy.136
  143.9 6.2 %fusion.78 = f32[1536,1,128]{0,2,1:T(8,128)} fusion(f32[1536,1,128]{0,2,1:T(8,128)} %copy.133, f32[1536,512,2]{1,0,2:T(8,128)} %copy-done.2, f32[2,512]{1,0:T(2,128)S(1)} %fusion.77, f32[2,512]{1,0:T(2,128)S(1)} %get-tuple-element.360, pred[512,1536]{0,1:T(8,128)(4,1)} %copy-done.3, bf16[512,2,128]{2,1,0:T(2,128)(2,1)S(1)} %copy-done.6), kind=kOutput, calls=%fused_computation.23.clone.1 | convolution fusion | flops 410714112 | bytes 8921088 | tf_op jit(solution)/shard_map/while/body/eval_jaxpr/agqk,qagd->kad/dot_general | solution.py:37
  152.4 2.7 constant_dynamic-update-slice_fusion.3
  155.1 2.3 fusion.82
  161.7 2.4 fusion.76
  166.9 3.5 fusion.79
  177.0 3.2 fusion.81
  180.2 2.4 copy.136
  186.9 6.2 %fusion.78 = f32[1536,1,128]{0,2,1:T(8,128)} fusion(f32[1536,1,128]{0,2,1:T(8,128)} %copy.133, f32[1536,512,2]{1,0,2:T(8,128)} %copy-done.2, f32[2,512]{1,0:T(2,128)S(1)} %fusion.77, f32[2,512]{1,0:T(2,128)S(1)} %get-tuple-element.360, pred[512,1536]{0,1:T(8,128)(4,1)} %copy-done.3, bf16[512,2,128]{2,1,0:T(2,128)(2,1)S(1)} %copy-done.6), kind=kOutput, calls=%fused_computation.23.clone.1 | convolution fusion | flops 410714112 | bytes 8921088 | tf_op jit(solution)/shard_map/while/body/eval_jaxpr/agqk,qagd->kad/dot_general | solution.py:37
  195.4 2.7 constant_dynamic-update-slice_fusion.3
  198.1 2.3 fusion.82
  204.7 2.4 fusion.76
  209.9 3.5 fusion.79
  220.1 3.2 fusion.81
  223.3 2.4 copy.136
  230.0 6.2 %fusion.78 = f32[1536,1,128]{0,2,1:T(8,128)} fusion(f32[1536,1,128]{0,2,1:T(8,128)} %copy.133, f32[1536,512,2]{1,0,2:T(8,128)} %copy-done.2, f32[2,512]{1,0:T(2,128)S(1)} %fusion.77, f32[2,512]{1,0:T(2,128)S(1)} %get-tuple-element.360, pred[512,1536]{0,1:T(8,128)(4,1)} %copy-done.3, bf16[512,2,128]{2,1,0:T(2,128)(2,1)S(1)} %copy-done.6), kind=kOutput, calls=%fused_computation.23.clone.1 | convolution fusion | flops 410714112 | bytes 8921088 | tf_op jit(solution)/shard_map/while/body/eval_jaxpr/agqk,qagd->kad/dot_general | solution.py:37
  238.5 2.6 constant_dynamic-update-slice_fusion.3
  241.1 2.3 fusion.82
  247.7 2.4 fusion.76
  252.9 3.5 fusion.79
  263.0 3.2 fusion.81
  266.2 2.4 copy.136
  272.9 6.2 %fusion.78 = f32[1536,1,128]{0,2,1:T(8,128)} fusion(f32[1536,1,128]{0,2,1:T(8,128)} %copy.133, f32[1536,512,2]{1,0,2:T(8,128)} %copy-done.2, f32[2,512]{1,0:T(2,128)S(1)} %fusion.77, f32[2,512]{1,0:T(2,128)S(1)} %get-tuple-element.360, pred[512,1536]{0,1:T(8,128)(4,1)} %copy-done.3, bf16[512,2,128]{2,1,0:T(2,128)(2,1)S(1)} %copy-done.6), kind=kOutput, calls=%fused_computation.23.clone.1 | convolution fusion | flops 410714112 | bytes 8921088 | tf_op jit(solution)/shard_map/while/body/eval_jaxpr/agqk,qagd->kad/dot_general | solution.py:37
  281.4 2.6 constant_dynamic-update-slice_fusion.3
  284.1 2.3 fusion.82
  290.7 2.4 fusion.76
  295.8 3.5 fusion.79
  306.0 3.2 fusion.81
  309.2 2.4 copy.136
  315.9 6.2 %fusion.78 = f32[1536,1,128]{0,2,1:T(8,128)} fusion(f32[1536,1,128]{0,2,1:T(8,128)} %copy.133, f32[1536,512,2]{1,0,2:T(8,128)} %copy-done.2, f32[2,512]{1,0:T(2,128)S(1)} %fusion.77, f32[2,512]{1,0:T(2,128)S(1)} %get-tuple-element.360, pred[512,1536]{0,1:T(8,128)(4,1)} %copy-done.3, bf16[512,2,128]{2,1,0:T(2,128)(2,1)S(1)} %copy-done.6), kind=kOutput, calls=%fused_computation.23.clone.1 | convolution fusion | flops 410714112 | bytes 8921088 | tf_op jit(solution)/shard_map/while/body/eval_jaxpr/agqk,qagd->kad/dot_general | solution.py:37
  324.4 2.6 constant_dynamic-update-slice_fusion.3
  327.0 2.3 fusion.82
  333.6 2.4 fusion.76
  338.8 3.5 fusion.79
  349.0 3.2 fusion.81
  352.1 2.4 copy.136
  358.9 6.2 %fusion.78 = f32[1536,1,128]{0,2,1:T(8,128)} fusion(f32[1536,1,128]{0,2,1:T(8,128)} %copy.133, f32[1536,512,2]{1,0,2:T(8,128)} %copy-done.2, f32[2,512]{1,0:T(2,128)S(1)} %fusion.77, f32[2,512]{1,0:T(2,128)S(1)} %get-tuple-element.360, pred[512,1536]{0,1:T(8,128)(4,1)} %copy-done.3, bf16[512,2,128]{2,1,0:T(2,128)(2,1)S(1)} %copy-done.6), kind=kOutput, calls=%fused_computation.23.clone.1 | convolution fusion | flops 410714112 | bytes 8921088 | tf_op jit(solution)/shard_map/while/body/eval_jaxpr/agqk,qagd->kad/dot_general | solution.py:37
  367.4 2.6 constant_dynamic-update-slice_fusion.3
  370.0 2.3 fusion.82
  376.1 13.7 %collective-permute-done.1 = bf16[2,1024,1,128]{3,1,2,0:T(8,128)(2,1)S(1)} collective-permute-done((bf16[2,1024,1,128]{3,1,2,0:T(8,128)(2,1)S(1)}, bf16[2,1024,1,128]{3,1,2,0:T(8,128)(2,1)S(1)}, u32[]{:S(2)}, u32[]{:S(2)}) %collective-permute-start.1) | collective-permute-done | bytes 524320 | tf_op jit(solution)/shard_map/ppermute | solution.py:14
  391.9 5.4 %all-to-all-start.6 = ((bf16[16,192,128]{2,1,0:T(8,128)(2,1)}), bf16[16,192,128]{2,1,0:T(8,128)(2,1)S(1)}, u32[]{:S(2)}, u32[]{:S(2)}) async-start(bf16[16,192,128]{2,1,0:T(8,128)(2,1)} %bitcast.23), calls=%async_computation.6 | async-start | bytes 1572864 | tf_op jit(solution)/shard_map/all_to_all | solution.py:152
  398.3 11.5 %all-to-all-done.6 = bf16[16,192,128]{2,1,0:T(8,128)(2,1)S(1)} async-done(((bf16[16,192,128]{2,1,0:T(8,128)(2,1)}), bf16[16,192,128]{2,1,0:T(8,128)(2,1)S(1)}, u32[]{:S(2)}, u32[]{:S(2)}) %all-to-all-start.6) | async-done | bytes 786464 | tf_op jit(solution)/shard_map/all_to_all | solution.py:152
  409.8 6.3 %all-to-all-start.5 = ((bf16[16,192,128]{2,1,0:T(8,128)(2,1)}), bf16[16,192,128]{2,1,0:T(8,128)(2,1)S(1)}, u32[]{:S(2)}, u32[]{:S(2)}) async-start(bf16[16,192,128]{2,1,0:T(8,128)(2,1)} %bitcast.18), calls=%async_computation.5 | async-start | bytes 1572864 | tf_op jit(solution)/shard_map/all_to_all | solution.py:149
  416.1 3.6 copy.71
  422.0 6.6 %all-to-all-done.5 = bf16[16,192,128]{2,1,0:T(8,128)(2,1)S(1)} async-done(((bf16[16,192,128]{2,1,0:T(8,128)(2,1)}), bf16[16,192,128]{2,1,0:T(8,128)(2,1)S(1)}, u32[]{:S(2)}, u32[]{:S(2)}) %all-to-all-start.5) | async-done | bytes 786464 | tf_op jit(solution)/shard_map/all_to_all | solution.py:149
  429.4 6.4 %all-to-all-start.4 = ((bf16[16,192,256]{2,1,0:T(8,128)(2,1)}), bf16[16,192,256]{2,1,0:T(8,128)(2,1)S(1)}, u32[]{:S(2)}, u32[]{:S(2)}) async-start(bf16[16,192,256]{2,1,0:T(8,128)(2,1)} %convert_element_type.57), calls=%async_computation.4 | async-start | bytes 3145728 | tf_op jit(solution)/shard_map/all_to_all | solution.py:146
  439.0 17.7 %all-to-all-done.4 = bf16[16,192,256]{2,1,0:T(8,128)(2,1)S(1)} async-done(((bf16[16,192,256]{2,1,0:T(8,128)(2,1)}), bf16[16,192,256]{2,1,0:T(8,128)(2,1)S(1)}, u32[]{:S(2)}, u32[]{:S(2)}) %all-to-all-start.4) | async-done | bytes 1572896 | tf_op jit(solution)/shard_map/all_to_all | solution.py:146
  (195 shorter events, 146.7 us)
Async XLA Ops:
  0.6 1.1 copy-start
  0.6 10.6 %copy-start.10 = (bf16[192,2048]{1,0:T(8,128)(2,1)S(1)}, bf16[192,2048]{1,0:T(8,128)(2,1)}, u32[]{:S(2)}) copy-start(bf16[192,2048]{1,0:T(8,128)(2,1)} %param.8) | copy-start | bytes 2359300
  2.9 20.8 %all-to-all-start.2 = ((bf16[192,16,128]{2,0,1:T(8,128)(2,1)}), bf16[192,16,128]{2,0,1:T(8,128)(2,1)S(1)}, u32[]{:S(2)}, u32[]{:S(2)}) async-start(bf16[192,16,128]{2,0,1:T(8,128)(2,1)} %copy_bitcast_fusion.4), calls=%async_computation.2 | async-start | bytes 1572864 | tf_op jit(solution)/shard_map/all_to_all | solution.py:134
  23.7 28.8 %copy-start.7 = (bf16[192,16,128]{2,0,1:T(8,128)(2,1)}, bf16[192,16,128]{2,0,1:T(8,128)(2,1)S(1)}, u32[]{:S(2)}) copy-start(bf16[192,16,128]{2,0,1:T(8,128)(2,1)S(1)} %all-to-all-done.2) | copy-start | bytes 2359300
  23.7 18.7 %all-to-all-start.1 = ((bf16[192,16,128]{2,0,1:T(8,128)(2,1)}), bf16[192,16,128]{2,0,1:T(8,128)(2,1)S(1)}, u32[]{:S(2)}, u32[]{:S(2)}) async-start(bf16[192,16,128]{2,0,1:T(8,128)(2,1)} %copy_bitcast_fusion.5), calls=%async_computation.1 | async-start | bytes 1572864 | tf_op jit(solution)/shard_map/all_to_all | solution.py:133
  42.4 0.9 copy-start.8
  43.3 27.3 %all-to-all-start = ((bf16[192,16,256]{2,0,1:T(8,128)(2,1)}), bf16[192,16,256]{2,0,1:T(8,128)(2,1)S(1)}, u32[]{:S(2)}, u32[]{:S(2)}) async-start(bf16[192,16,256]{2,0,1:T(8,128)(2,1)} %bitcast.161), calls=%async_computation | async-start | bytes 3145728 | tf_op jit(solution)/shard_map/all_to_all | solution.py:132
  52.5 30.7 %copy-start.11 = (s32[16]{0:T(128)S(1)}, s32[16]{0:T(128)}, u32[]{:S(2)}) copy-start(s32[16]{0:T(128)} %param.11) | copy-start | bytes 196
  70.6 38.9 %all-to-all-start.3 = ((bf16[192,16,256]{2,0,1:T(8,128)(2,1)}), bf16[192,16,256]{2,0,1:T(8,128)(2,1)S(1)}, u32[]{:S(2)}, u32[]{:S(2)}) async-start(bf16[192,16,256]{2,0,1:T(8,128)(2,1)} %bitcast.160), calls=%async_computation.3 | async-start | bytes 3145728 | tf_op jit(solution)/shard_map/all_to_all | solution.py:135
  79.2 14.4 %collective-permute-start = (bf16[2,1024,1,128]{3,1,2,0:T(8,128)(2,1)}, bf16[2,1024,1,128]{3,1,2,0:T(8,128)(2,1)}, u32[]{:S(2)}, u32[]{:S(2)}) collective-permute-start(bf16[2,1024,1,128]{3,1,2,0:T(8,128)(2,1)} %pad_maximum_fusion.4), channel_id=1, source_target_pairs={{0,16},{16,32},{32,48},{48,64},{64,80},{80,96},{96,112},{1,17},{17... | collective-permute-start | bytes 1572872 | tf_op jit(solution)/shard_map/ppermute | solution.py:14
  117.3 10.0 %copy-start.3 = (pred[512,1536]{0,1:T(8,128)(4,1)}, pred[512,1536]{0,1:T(8,128)(4,1)S(1)}, u32[]{:S(2)}) copy-start(pred[512,1536]{0,1:T(8,128)(4,1)S(1)} %fusion.75) | copy-start | bytes 2359300 | tf_op jit(solution)/shard_map/while
  121.0 6.3 %copy-start.2 = (f32[1536,512,2]{1,0,2:T(8,128)}, f32[1536,512,2]{1,0,2:T(8,128)S(1)}, u32[]{:S(2)}) copy-start(f32[1536,512,2]{1,0,2:T(8,128)S(1)} %get-tuple-element.359) | copy-start | bytes 18874372 | tf_op jit(solution)/shard_map/while
  123.8 3.5 copy-start.5
  137.2 6.7 %copy-start.6 = (bf16[512,2,128]{2,1,0:T(2,128)(2,1)S(1)}, bf16[512,2,128]{2,1,0:T(2,128)(2,1)}, u32[]{:S(2)}) copy-start(bf16[512,2,128]{2,1,0:T(2,128)(2,1)} %copy-done.5) | copy-start | bytes 786436 | tf_op jit(solution)/shard_map/while
  160.3 10.0 %copy-start.3 = (pred[512,1536]{0,1:T(8,128)(4,1)}, pred[512,1536]{0,1:T(8,128)(4,1)S(1)}, u32[]{:S(2)}) copy-start(pred[512,1536]{0,1:T(8,128)(4,1)S(1)} %fusion.75) | copy-start | bytes 2359300 | tf_op jit(solution)/shard_map/while
  164.0 6.3 %copy-start.2 = (f32[1536,512,2]{1,0,2:T(8,128)}, f32[1536,512,2]{1,0,2:T(8,128)S(1)}, u32[]{:S(2)}) copy-start(f32[1536,512,2]{1,0,2:T(8,128)S(1)} %get-tuple-element.359) | copy-start | bytes 18874372 | tf_op jit(solution)/shard_map/while
  166.8 3.5 copy-start.5
  180.2 6.7 %copy-start.6 = (bf16[512,2,128]{2,1,0:T(2,128)(2,1)S(1)}, bf16[512,2,128]{2,1,0:T(2,128)(2,1)}, u32[]{:S(2)}) copy-start(bf16[512,2,128]{2,1,0:T(2,128)(2,1)} %copy-done.5) | copy-start | bytes 786436 | tf_op jit(solution)/shard_map/while
  203.4 10.0 %copy-start.3 = (pred[512,1536]{0,1:T(8,128)(4,1)}, pred[512,1536]{0,1:T(8,128)(4,1)S(1)}, u32[]{:S(2)}) copy-start(pred[512,1536]{0,1:T(8,128)(4,1)S(1)} %fusion.75) | copy-start | bytes 2359300 | tf_op jit(solution)/shard_map/while
  207.1 6.3 %copy-start.2 = (f32[1536,512,2]{1,0,2:T(8,128)}, f32[1536,512,2]{1,0,2:T(8,128)S(1)}, u32[]{:S(2)}) copy-start(f32[1536,512,2]{1,0,2:T(8,128)S(1)} %get-tuple-element.359) | copy-start | bytes 18874372 | tf_op jit(solution)/shard_map/while
  209.9 3.5 copy-start.5
  223.2 6.7 %copy-start.6 = (bf16[512,2,128]{2,1,0:T(2,128)(2,1)S(1)}, bf16[512,2,128]{2,1,0:T(2,128)(2,1)}, u32[]{:S(2)}) copy-start(bf16[512,2,128]{2,1,0:T(2,128)(2,1)} %copy-done.5) | copy-start | bytes 786436 | tf_op jit(solution)/shard_map/while
  246.4 10.0 %copy-start.3 = (pred[512,1536]{0,1:T(8,128)(4,1)}, pred[512,1536]{0,1:T(8,128)(4,1)S(1)}, u32[]{:S(2)}) copy-start(pred[512,1536]{0,1:T(8,128)(4,1)S(1)} %fusion.75) | copy-start | bytes 2359300 | tf_op jit(solution)/shard_map/while
  250.1 6.3 %copy-start.2 = (f32[1536,512,2]{1,0,2:T(8,128)}, f32[1536,512,2]{1,0,2:T(8,128)S(1)}, u32[]{:S(2)}) copy-start(f32[1536,512,2]{1,0,2:T(8,128)S(1)} %get-tuple-element.359) | copy-start | bytes 18874372 | tf_op jit(solution)/shard_map/while
  252.9 3.5 copy-start.5
  266.2 6.7 %copy-start.6 = (bf16[512,2,128]{2,1,0:T(2,128)(2,1)S(1)}, bf16[512,2,128]{2,1,0:T(2,128)(2,1)}, u32[]{:S(2)}) copy-start(bf16[512,2,128]{2,1,0:T(2,128)(2,1)} %copy-done.5) | copy-start | bytes 786436 | tf_op jit(solution)/shard_map/while
  289.3 10.0 %copy-start.3 = (pred[512,1536]{0,1:T(8,128)(4,1)}, pred[512,1536]{0,1:T(8,128)(4,1)S(1)}, u32[]{:S(2)}) copy-start(pred[512,1536]{0,1:T(8,128)(4,1)S(1)} %fusion.75) | copy-start | bytes 2359300 | tf_op jit(solution)/shard_map/while
  293.0 6.3 %copy-start.2 = (f32[1536,512,2]{1,0,2:T(8,128)}, f32[1536,512,2]{1,0,2:T(8,128)S(1)}, u32[]{:S(2)}) copy-start(f32[1536,512,2]{1,0,2:T(8,128)S(1)} %get-tuple-element.359) | copy-start | bytes 18874372 | tf_op jit(solution)/shard_map/while
  295.8 3.5 copy-start.5
  309.2 6.7 %copy-start.6 = (bf16[512,2,128]{2,1,0:T(2,128)(2,1)S(1)}, bf16[512,2,128]{2,1,0:T(2,128)(2,1)}, u32[]{:S(2)}) copy-start(bf16[512,2,128]{2,1,0:T(2,128)(2,1)} %copy-done.5) | copy-start | bytes 786436 | tf_op jit(solution)/shard_map/while
  332.3 10.0 %copy-start.3 = (pred[512,1536]{0,1:T(8,128)(4,1)}, pred[512,1536]{0,1:T(8,128)(4,1)S(1)}, u32[]{:S(2)}) copy-start(pred[512,1536]{0,1:T(8,128)(4,1)S(1)} %fusion.75) | copy-start | bytes 2359300 | tf_op jit(solution)/shard_map/while
  336.0 6.3 %copy-start.2 = (f32[1536,512,2]{1,0,2:T(8,128)}, f32[1536,512,2]{1,0,2:T(8,128)S(1)}, u32[]{:S(2)}) copy-start(f32[1536,512,2]{1,0,2:T(8,128)S(1)} %get-tuple-element.359) | copy-start | bytes 18874372 | tf_op jit(solution)/shard_map/while
  338.8 3.5 copy-start.5
  352.1 6.7 %copy-start.6 = (bf16[512,2,128]{2,1,0:T(2,128)(2,1)S(1)}, bf16[512,2,128]{2,1,0:T(2,128)(2,1)}, u32[]{:S(2)}) copy-start(bf16[512,2,128]{2,1,0:T(2,128)(2,1)} %copy-done.5) | copy-start | bytes 786436 | tf_op jit(solution)/shard_map/while
  372.3 2.2 copy-start.4
  374.7 15.0 %collective-permute-start.1 = (bf16[2,1024,1,128]{3,1,2,0:T(8,128)(2,1)S(1)}, bf16[2,1024,1,128]{3,1,2,0:T(8,128)(2,1)S(1)}, u32[]{:S(2)}, u32[]{:S(2)}) collective-permute-start(bf16[2,1024,1,128]{3,1,2,0:T(8,128)(2,1)S(1)} %pad_maximum_fusion.5), channel_id=1, source_target_pairs={{16,0},{32,16},{48,32},{64,48},{80,64},{96,80},{112,96},{17,1},{33... | collective-permute-start | bytes 1572872 | tf_op jit(solution)/shard_map/ppermute | solution.py:14
  391.9 17.9 %all-to-all-start.6 = ((bf16[16,192,128]{2,1,0:T(8,128)(2,1)}), bf16[16,192,128]{2,1,0:T(8,128)(2,1)S(1)}, u32[]{:S(2)}, u32[]{:S(2)}) async-start(bf16[16,192,128]{2,1,0:T(8,128)(2,1)} %bitcast.23), calls=%async_computation.6 | async-start | bytes 1572864 | tf_op jit(solution)/shard_map/all_to_all | solution.py:152
  409.8 18.7 %all-to-all-start.5 = ((bf16[16,192,128]{2,1,0:T(8,128)(2,1)}), bf16[16,192,128]{2,1,0:T(8,128)(2,1)S(1)}, u32[]{:S(2)}, u32[]{:S(2)}) async-start(bf16[16,192,128]{2,1,0:T(8,128)(2,1)} %bitcast.18), calls=%async_computation.5 | async-start | bytes 1572864 | tf_op jit(solution)/shard_map/all_to_all | solution.py:149
  428.5 0.9 copy-start.9
  429.4 27.3 %all-to-all-start.4 = ((bf16[16,192,256]{2,1,0:T(8,128)(2,1)}), bf16[16,192,256]{2,1,0:T(8,128)(2,1)S(1)}, u32[]{:S(2)}, u32[]{:S(2)}) async-start(bf16[16,192,256]{2,1,0:T(8,128)(2,1)} %convert_element_type.57), calls=%async_computation.4 | async-start | bytes 3145728 | tf_op jit(solution)/shard_map/all_to_all | solution.py:146
  435.9 22.2 %copy-start.1 = (bf16[192,2048]{1,0:T(8,128)(2,1)S(1)}, bf16[192,2048]{1,0:T(8,128)(2,1)}, u32[]{:S(2)}) copy-start(bf16[192,2048]{1,0:T(8,128)(2,1)} %param.9) | copy-start | bytes 2359300
where the time goes:
time: 467 us; the launch traced here: 458 us
  local copies, waits for them, and re-layouts  147 us (31%)
  waiting for transfers between devices  109 us (23%)
  matrix products  105 us (22%)
  starting transfers between devices  51.4 us (11%)
  other arithmetic  40.8 us (9%)
    dot_general x6, matrix products, tile_grads(): jnp.einsum('agqk,qagd->kad', weights_b, out_four, preferred_element_type=...  37.4 us
    dynamic_update_slice x12, local copies, waits for them, and re-layouts, advance(): lax.dynamic_update_slice_in_dim(value_total, lax.dynamic_slice_in_dim(val...  29.5 us
    dynamic_slice x12, local copies, waits for them, and re-layouts, advance(): lax.dynamic_slice_in_dim(key_total, key_first, span, 0) + grad_keys  26.1 us
    dynamic_slice x12, local copies, waits for them, and re-layouts, advance(): lax.dynamic_slice_in_dim(value_total, key_first, span, 0) + grad_values  26.1 us
    ppermute x2, waiting for transfers between devices, passed_along(): return lax.ppermute(shard, axis, pairs)  23.6 us
    dot_general x6, matrix products, tile_grads(): jnp.einsum('qagd,kad->agqk', out_four, value_rows, preferred_element_type...  20.9 us
    dot_general x6, matrix products, tile_grads(): jnp.einsum('agqk,qagd->kad', grad_scores, q_four, preferred_element_type=...  19.1 us
    all_to_all x1, waiting for transfers between devices, local(): lax.all_to_all(queries, 'head', split_axis=1, concat_axis=0, tiled=True)  18.1 us
  transfers between devices with their start and end apart: 9, of which 9 were waited for; matrix products, arithmetic and copies ran while one was open for 5% of the time, Pallas kernels for 0%

commit v1 on v0

v1 whole, which is shorter than its diff:
```python
import jax
import jax.numpy as jnp
from jax import lax
from jax.experimental import pallas as pl
from jax.experimental.pallas import tpu as pltpu
from jax.sharding import PartitionSpec as P

HD = 128
WINDOW = 1024
BQ = 256
BK = 256
NT=(WINDOW+BQ)//BK
SCALE=HD**-0.5
C2=SCALE*1.4426950408889634
NEG=-1e30
f32 = jnp.float32
bf16 = jnp.bfloat16
NTK=(((1,),(1,)),((),()))
NN=(((1,),(0,)),((),()))

def block(b, base, len_ref, q, do, k_ref, v_ref, kt_ref, dk_ref, dv_ref, s_scr, p_scr):
    first = base + b*BQ - WINDOW
    qi = lax.broadcasted_iota(jnp.int32,(1,BQ),1)
    gpos = first + WINDOW + qi
    end = jnp.int32(0)
    start = jnp.zeros((1,BQ),jnp.int32)
    for d in range(16):
        end = end + len_ref[d]
        start = jnp.where(gpos >= end, end, start)
    lo = jnp.maximum(qi+1, start-first)
    ki = lax.broadcasted_iota(jnp.int32,(BK,BQ),0)
    m = None
    for t in range(NT):
        r = pl.multiple_of(b*BQ + t*BK, BK)
        s = lax.dot_general(k_ref[pl.ds(r,BK),:], q, NTK, preferred_element_type=f32)
        ok = ki >= lo - t*BK
        if t==NT-1:
            ok = ok & (ki <= lax.broadcasted_iota(jnp.int32,(BK,BQ),1))
        s = jnp.where(ok, s, NEG)
        s_scr[t] = s
        mt = jnp.max(s.reshape(BK//8,8,BQ),axis=0)
        m = mt if m is None else jnp.maximum(m,mt)
    m = jnp.max(m,axis=0,keepdims=True)
    l = jnp.zeros((8,BQ),f32); dd = jnp.zeros((8,BQ),f32)
    for t in range(NT):
        r = pl.multiple_of(b*BQ + t*BK, BK)
        p = jnp.exp2((s_scr[t]-m)*C2)
        s_scr[t] = p
        dp = lax.dot_general(v_ref[pl.ds(r,BK),:], do, NTK, preferred_element_type=f32)
        p_scr[t] = dp
        l = l + jnp.sum(p.reshape(BK//8,8,BQ),axis=0)
        dd = dd + jnp.sum((p*dp).reshape(BK//8,8,BQ),axis=0)
    l = jnp.sum(l,axis=0,keepdims=True); dd = jnp.sum(dd,axis=0,keepdims=True)
    inv = 1.0/l
    dd = dd*inv
    dqt = None
    for t in range(NT):
        r = pl.multiple_of(b*BQ + t*BK, BK)
        w = s_scr[t]*inv
        ds = (w*(p_scr[t]-dd)).astype(bf16)
        dv_ref[pl.ds(r,BK),:] += lax.dot_general(w.astype(bf16), do, NN, preferred_element_type=f32)
        dk_ref[pl.ds(r,BK),:] += lax.dot_general(ds, q, NN, preferred_element_type=f32)
        x = lax.dot_general(kt_ref[:,pl.ds(r,BK)], ds, NN, preferred_element_type=f32)
        dqt = x if dqt is None else dqt + x
    return (dqt*SCALE).T


def attention_kernel(len_ref, q_ref, k_ref, v_ref, do_ref, dq_ref, dk_out, dv_out, kt, dk, dv, s_scr, p_scr):
    group = q_ref.shape[0]
    base = lax.axis_index("seq") * group

    def prepare(i, carry):
        r = pl.multiple_of(i * BK, BK)
        kt[:, pl.ds(r, BK)] = k_ref[pl.ds(r, BK), :].T
        dk[pl.ds(r, BK), :] = jnp.zeros((BK, HD), f32)
        dv[pl.ds(r, BK), :] = jnp.zeros((BK, HD), f32)
        return carry

    lax.fori_loop(0, k_ref.shape[0] // BK, prepare, 0)
    for h in range(q_ref.shape[1] // HD):
        cols = pl.ds(h * HD, HD)

        def tile(b, carry):
            r = pl.multiple_of(b * BQ, BQ)
            rows = pl.ds(r, BQ)
            q = q_ref[rows, cols]
            do = do_ref[rows, cols]
            grad = block(b, base, len_ref, q, do, k_ref, v_ref, kt, dk, dv, s_scr, p_scr)
            dq_ref[rows, cols] = grad.astype(bf16)
            return carry

        lax.fori_loop(0, group // BQ, tile, 0)
    dk_out[...] = (dk[...] * SCALE).astype(bf16)
    dv_out[...] = dv[...].astype(bf16)


def passed_along(shard, axis, by):
    count = lax.axis_size(axis)
    pairs = [(i, i + by) for i in range(count) if 0 <= i + by < count]
    return lax.ppermute(shard, axis, pairs)


def local(queries, keys, values, grad_out, doc_lengths):
    def heads(x):
        return lax.all_to_all(x, "head", split_axis=1, concat_axis=0, tiled=True)

    def tokens(x):
        return lax.all_to_all(x, "head", split_axis=0, concat_axis=1, tiled=True)

    q, k, v, do = heads(queries), heads(keys), heads(values), heads(grad_out)
    group = q.shape[0]
    rims = passed_along(jnp.concatenate([k[group - WINDOW :], v[group - WINDOW :]], axis=1), "seq", 1)
    k_ext = jnp.concatenate([rims[:, :HD], k], axis=0)
    v_ext = jnp.concatenate([rims[:, HD:], v], axis=0)
    vmem = pl.BlockSpec(memory_space=pltpu.VMEM)
    dq, dk, dv = pl.pallas_call(
        attention_kernel,
        out_shape=(
            jax.ShapeDtypeStruct(q.shape, bf16),
            jax.ShapeDtypeStruct(k_ext.shape, bf16),
            jax.ShapeDtypeStruct(v_ext.shape, bf16),
        ),
        in_specs=[pl.BlockSpec(memory_space=pltpu.SMEM), vmem, vmem, vmem, vmem],
        out_specs=(vmem, vmem, vmem),
        scratch_shapes=[
            pltpu.VMEM((HD, k_ext.shape[0]), bf16),
            pltpu.VMEM(k_ext.shape, f32),
            pltpu.VMEM(k_ext.shape, f32),
            pltpu.VMEM((NT, BK, BQ), f32),
            pltpu.VMEM((NT, BK, BQ), f32),
        ],
        compiler_params=pltpu.CompilerParams(vmem_limit_bytes=48 << 20),
    )(doc_lengths, q, k_ext, v_ext, do)
    back = passed_along(jnp.concatenate([dk[:WINDOW], dv[:WINDOW]], axis=1), "seq", -1).astype(f32)
    own = [dk[WINDOW:], dv[WINDOW:]]
    full = []
    for i, grad in enumerate(own):
        tail = grad[group - WINDOW :].astype(f32) + back[:, i * HD : (i + 1) * HD]
        full.append(jnp.concatenate([grad[: group - WINDOW], tail.astype(bf16)], axis=0))
    return tokens(dq), tokens(full[0]), tokens(full[1])


def solution(mesh):
    rows = P(("seq", "head"), None)
    return jax.shard_map(
        local,
        mesh=mesh,
        in_specs=(rows, rows, rows, rows, P()),
        out_specs=(rows, rows, rows),
        check_vma=False,
    )
```

time: 467 us -> 233 us (0.50); the launches traced: 458 us -> 230 us
  local copies, waits for them, and re-layouts: 147 us -> 15.7 us
  matrix products: 105 us -> 0 us
  other arithmetic: 40.8 us -> 1.42 us
  Pallas kernels: 0 us -> 37.6 us
  blocking collectives: 0 us -> 18.7 us
  starting transfers between devices: 51.4 us -> 44.2 us
    dot_general x30 -> x0, matrix products: 105 us -> none  [the longest x6 37.4 us: tile_grads(): jnp.einsum('agqk,qagd->kad', weights_b, out_four, preferred_element_type=...]
    dynamic_slice x54 -> x0, local copies, waits for them, and re-layouts: 72.6 us -> none  [the longest x12 26.1 us: advance(): lax.dynamic_slice_in_dim(key_total, key_first, span, 0) + grad_keys]
    dynamic_update_slice x18 -> x0, local copies, waits for them, and re-layouts: 43.7 us -> none  [the longest x12 29.5 us: advance(): lax.dynamic_update_slice_in_dim(value_total, lax.dynamic_slice_in_dim(val...]
    pallas_call x0 -> x1, Pallas kernels: none -> 37.6 us  [local(): pl.pallas_call(attention_kernel, out_shape=(jax.ShapeDtypeStruct(q.shape,...]
    all_to_all x0 -> x1, blocking collectives: none -> 18.7 us  [tokens(): return lax.all_to_all(x, 'head', split_axis=0, concat_axis=1, tiled=True)]
    another operation x12 -> x0, other arithmetic: 16.7 us -> none
    and x6 -> x0, other arithmetic: 9.2 us -> none  [advance(): allowed & (q_pos[:, None] - k_pos[None, :] < WINDOW) & (k_pos[None, :] >= 0)]
    reduce_sum x8 -> x0, other arithmetic: 8.89 us -> none  [the longest x6 8.66 us: tile_grads(): weights = exponent / jnp.sum(exponent, axis=3, keepdims=True)]
  transfers between devices with their start and end apart: 9 -> 8, of which waited for: 9 -> 8; matrix products, arithmetic and copies ran while one was open for 5% -> 4% of each run, Pallas kernels for 0% -> 0%
where the time goes in v1:
time: 233 us; the launch traced here: 230 us
  waiting for transfers between devices  111 us (48%)
  starting transfers between devices  44.2 us (19%)
  Pallas kernels  37.6 us (16%)
  blocking collectives  18.7 us (8%)
  local copies, waits for them, and re-layouts  15.7 us (7%)
    all_to_all x4, waiting for transfers between devices, heads(): return lax.all_to_all(x, 'head', split_axis=1, concat_axis=0, tiled=True)  55.8 us
    pallas_call x1, Pallas kernels, local(): pl.pallas_call(attention_kernel, out_shape=(jax.ShapeDtypeStruct(q.shape,...  37.6 us
    all_to_all x2, waiting for transfers between devices, tokens(): return lax.all_to_all(x, 'head', split_axis=0, concat_axis=1, tiled=True)  30.8 us
    all_to_all x4, starting transfers between devices, heads(): return lax.all_to_all(x, 'head', split_axis=1, concat_axis=0, tiled=True)  28.2 us
    ppermute x2, waiting for transfers between devices, passed_along(): return lax.ppermute(shard, axis, pairs)  24.5 us
    all_to_all x1, blocking collectives, tokens(): return lax.all_to_all(x, 'head', split_axis=0, concat_axis=1, tiled=True)  18.7 us
    all_to_all x2, starting transfers between devices, tokens(): return lax.all_to_all(x, 'head', split_axis=0, concat_axis=1, tiled=True)  11.4 us
    all_to_all x4, local copies, waits for them, and re-layouts, heads(): return lax.all_to_all(x, 'head', split_axis=1, concat_axis=0, tiled=True)  7.62 us
  transfers between devices with their start and end apart: 8, of which 8 were waited for; matrix products, arithmetic and copies ran while one was open for 4% of the time, Pallas kernels for 0%

profile of v1, /device:TPU:7, one launch (start us, length us, event | category | flops | bytes accessed | tf_op | source)
XLA Modules:
  0.0 229.5 jit_solution(4975627871202538550)
XLA Ops:
  0.6 0.0 copy-start
  0.6 0.0 copy-start.10
  0.7 1.1 copy-done
  1.8 1.1 copy_bitcast_fusion.5
  2.9 8.4 %all-to-all-start.1 = ((bf16[192,16,128]{2,0,1:T(8,128)(2,1)}), bf16[192,16,128]{2,0,1:T(8,128)(2,1)S(1)}, u32[]{:S(2)}, u32[]{:S(2)}) async-start(bf16[192,16,128]{2,0,1:T(8,128)(2,1)} %copy_bitcast_fusion.5), calls=%async_computation.1 | async-start | bytes 1572864 | tf_op jit(solution)/shard_map/all_to_all | solution.py:105
  11.3 0.0 copy-done.10
  11.3 1.1 copy_bitcast_fusion.4
  12.4 11.3 %all-to-all-done.1 = bf16[192,16,128]{2,0,1:T(8,128)(2,1)S(1)} async-done(((bf16[192,16,128]{2,0,1:T(8,128)(2,1)}), bf16[192,16,128]{2,0,1:T(8,128)(2,1)S(1)}, u32[]{:S(2)}, u32[]{:S(2)}) %all-to-all-start.1) | async-done | bytes 786464 | tf_op jit(solution)/shard_map/all_to_all | solution.py:105
  23.7 0.0 copy-start.5
  23.7 6.3 %all-to-all-start.2 = ((bf16[192,16,128]{2,0,1:T(8,128)(2,1)}), bf16[192,16,128]{2,0,1:T(8,128)(2,1)S(1)}, u32[]{:S(2)}, u32[]{:S(2)}) async-start(bf16[192,16,128]{2,0,1:T(8,128)(2,1)} %copy_bitcast_fusion.4), calls=%async_computation.2 | async-start | bytes 1572864 | tf_op jit(solution)/shard_map/all_to_all | solution.py:105
  30.0 2.7 %copy.29 = bf16[24,16,8,256]{3,2,0,1:T(8,128)(2,1)} copy(bf16[24,16,8,256]{3,2,1,0:T(8,128)(2,1)} %bitcast.55) | data formatting | bytes 3145728 | tf_op jit(solution)/shard_map/all_to_all | solution.py:105
  32.7 9.7 %all-to-all-done.2 = bf16[192,16,128]{2,0,1:T(8,128)(2,1)S(1)} async-done(((bf16[192,16,128]{2,0,1:T(8,128)(2,1)}), bf16[192,16,128]{2,0,1:T(8,128)(2,1)S(1)}, u32[]{:S(2)}, u32[]{:S(2)}) %all-to-all-start.2) | async-done | bytes 786464 | tf_op jit(solution)/shard_map/all_to_all | solution.py:105
  42.4 0.0 copy-start.7
  42.4 0.9 copy-done.7
  43.3 6.4 %all-to-all-start = ((bf16[192,16,256]{2,0,1:T(8,128)(2,1)}), bf16[192,16,256]{2,0,1:T(8,128)(2,1)S(1)}, u32[]{:S(2)}, u32[]{:S(2)}) async-start(bf16[192,16,256]{2,0,1:T(8,128)(2,1)} %bitcast.47), calls=%async_computation | async-start | bytes 3145728 | tf_op jit(solution)/shard_map/all_to_all | solution.py:105
  49.8 2.7 %copy.28 = bf16[24,16,8,256]{3,2,0,1:T(8,128)(2,1)} copy(bf16[24,16,8,256]{3,2,1,0:T(8,128)(2,1)} %bitcast.56) | data formatting | bytes 3145728 | tf_op jit(solution)/shard_map/all_to_all | solution.py:105
  52.5 18.1 %all-to-all-done = bf16[192,16,256]{2,0,1:T(8,128)(2,1)S(1)} async-done(((bf16[192,16,256]{2,0,1:T(8,128)(2,1)}), bf16[192,16,256]{2,0,1:T(8,128)(2,1)S(1)}, u32[]{:S(2)}, u32[]{:S(2)}) %all-to-all-start) | async-done | bytes 1572896 | tf_op jit(solution)/shard_map/all_to_all | solution.py:105
  70.6 0.0 copy-start.4
  70.6 1.1 copy-done.4
  71.8 7.0 %all-to-all-start.3 = ((bf16[192,16,256]{2,0,1:T(8,128)(2,1)}), bf16[192,16,256]{2,0,1:T(8,128)(2,1)}, u32[]{:S(2)}, u32[]{:S(2)}) async-start(bf16[192,16,256]{2,0,1:T(8,128)(2,1)} %bitcast.46), calls=%async_computation.3 | async-start | bytes 3145728 | tf_op jit(solution)/shard_map/all_to_all | solution.py:105
  78.8 0.0 copy-done.5
  78.8 0.0 copy-start.8
  78.9 0.0 copy-start.6
  78.9 1.1 slice.55
  80.0 0.1 pad_maximum_fusion.4
  80.0 3.2 %collective-permute-start = (bf16[1024,256]{1,0:T(8,128)(2,1)S(1)}, bf16[1024,256]{1,0:T(8,128)(2,1)S(1)}, u32[]{:S(2)}, u32[]{:S(2)}) collective-permute-start(bf16[1024,256]{1,0:T(8,128)(2,1)S(1)} %pad_maximum_fusion.4), channel_id=1, source_target_pairs={{0,16},{16,32},{32,48},{48,64},{64,80},{80,96},{96,112},{1,17},{17... | collective-permute-start | bytes 1572872 | tf_op jit(solution)/shard_map/ppermute | solution.py:100
  83.3 10.9 %collective-permute-done = bf16[1024,256]{1,0:T(8,128)(2,1)S(1)} collective-permute-done((bf16[1024,256]{1,0:T(8,128)(2,1)S(1)}, bf16[1024,256]{1,0:T(8,128)(2,1)S(1)}, u32[]{:S(2)}, u32[]{:S(2)}) %collective-permute-start) | collective-permute-done | bytes 524320 | tf_op jit(solution)/shard_map/ppermute | solution.py:100
  94.2 0.0 copy-done.8
  94.2 0.0 copy-done.6
  94.2 0.0 copy-start.3
  94.2 0.1 pad_maximum_fusion
  94.4 16.6 %all-to-all-done.3 = bf16[192,16,256]{2,0,1:T(8,128)(2,1)} async-done(((bf16[192,16,256]{2,0,1:T(8,128)(2,1)}), bf16[192,16,256]{2,0,1:T(8,128)(2,1)}, u32[]{:S(2)}, u32[]{:S(2)}) %all-to-all-start.3) | async-done | bytes 1572896 | tf_op jit(solution)/shard_map/all_to_all | solution.py:105
  111.0 0.0 copy-done.3
  111.0 37.6 %shard_map.76 = (bf16[3072,256]{1,0:T(8,128)(2,1)}, bf16[4096,128]{1,0:T(8,128)(2,1)S(1)}, bf16[4096,128]{1,0:T(8,128)(2,1)S(1)}) custom-call(s32[16]{0:T(128)S(1)} %copy-done.3, bf16[3072,256]{1,0:T(8,128)(2,1)} %bitcast.49, bf16[4096,128]{1,0:T(8,128)(2,1)S(1)} %get-tuple-element.13.k_ref, bf16[4096,128]{1,0:T(8,128)(2,1)S(1)} %get-tuple-element.14.v_ref, ...), custom_call_target="tpu_custom_call" | custom-call | tf_op jit(solution)/shard_map/pallas_call | solution.py:116
  148.6 0.0 copy-start.1
  148.6 0.1 pad_maximum_fusion.5
  148.7 1.3 collective-permute-start.1
  150.0 13.6 %collective-permute-done.1 = bf16[1024,256]{1,0:T(8,128)(2,1)S(1)} collective-permute-done((bf16[1024,256]{1,0:T(8,128)(2,1)S(1)}, bf16[1024,256]{1,0:T(8,128)(2,1)S(1)}, u32[]{:S(2)}, u32[]{:S(2)}) %collective-permute-start.1) | collective-permute-done | bytes 524320 | tf_op jit(solution)/shard_map/ppermute | solution.py:100
  163.7 0.1 convert_element_type.16
  163.8 0.0 copy-done.1
  163.8 0.1 fusion
  163.9 0.0 copy-start.2
  163.9 0.9 pad_maximum_fusion.3
  164.8 5.5 %all-to-all-start.6 = ((bf16[16,192,128]{2,1,0:T(8,128)(2,1)}), bf16[16,192,128]{2,1,0:T(8,128)(2,1)S(1)}, u32[]{:S(2)}, u32[]{:S(2)}) async-start(bf16[16,192,128]{2,1,0:T(8,128)(2,1)} %bitcast.13), calls=%async_computation.6 | async-start | bytes 1572864 | tf_op jit(solution)/shard_map/all_to_all | solution.py:108
  170.4 0.0 copy-done.2
  170.4 0.1 pad_maximum_fusion.2
  170.5 12.3 %all-to-all-done.6 = bf16[16,192,128]{2,1,0:T(8,128)(2,1)S(1)} async-done(((bf16[16,192,128]{2,1,0:T(8,128)(2,1)}), bf16[16,192,128]{2,1,0:T(8,128)(2,1)S(1)}, u32[]{:S(2)}, u32[]{:S(2)}) %all-to-all-start.6) | async-done | bytes 786464 | tf_op jit(solution)/shard_map/all_to_all | solution.py:108
  182.8 18.7 %all_to_all.133 = bf16[16,192,128]{2,1,0:T(8,128)(2,1)} all-to-all(bf16[16,192,128]{2,1,0:T(8,128)(2,1)S(1)} %bitcast.54), channel_id=1, replica_groups=mesh['seq'=8,'head'=16] {'head'}, dimensions={0} | all-to-all | bytes 1572864 | tf_op jit(solution)/shard_map/all_to_all | solution.py:108
  201.4 5.9 %all-to-all-start.4 = ((bf16[16,192,256]{2,1,0:T(8,128)(2,1)}), bf16[16,192,256]{2,1,0:T(8,128)(2,1)S(1)}, u32[]{:S(2)}, u32[]{:S(2)}) async-start(bf16[16,192,256]{2,1,0:T(8,128)(2,1)} %bitcast.9), calls=%async_computation.4 | async-start | bytes 3145728 | tf_op jit(solution)/shard_map/all_to_all | solution.py:108
  207.3 0.0 copy-start.9
  207.3 1.0 copy_bitcast_fusion.2
  208.3 0.4 copy-done.9
  208.7 1.0 copy_bitcast_fusion.3
  209.7 18.5 %all-to-all-done.4 = bf16[16,192,256]{2,1,0:T(8,128)(2,1)S(1)} async-done(((bf16[16,192,256]{2,1,0:T(8,128)(2,1)}), bf16[16,192,256]{2,1,0:T(8,128)(2,1)S(1)}, u32[]{:S(2)}, u32[]{:S(2)}) %all-to-all-start.4) | async-done | bytes 1572896 | tf_op jit(solution)/shard_map/all_to_all | solution.py:108
  228.2 1.3 copy.19
  (6 shorter events, 0.2 us)
Async XLA Ops:
  0.6 1.1 copy-start
  0.6 10.6 %copy-start.10 = (bf16[192,2048]{1,0:T(8,128)(2,1)S(1)}, bf16[192,2048]{1,0:T(8,128)(2,1)}, u32[]{:S(2)}) copy-start(bf16[192,2048]{1,0:T(8,128)(2,1)} %param.7) | copy-start | bytes 2359300
  2.9 20.8 %all-to-all-start.1 = ((bf16[192,16,128]{2,0,1:T(8,128)(2,1)}), bf16[192,16,128]{2,0,1:T(8,128)(2,1)S(1)}, u32[]{:S(2)}, u32[]{:S(2)}) async-start(bf16[192,16,128]{2,0,1:T(8,128)(2,1)} %copy_bitcast_fusion.5), calls=%async_computation.1 | async-start | bytes 1572864 | tf_op jit(solution)/shard_map/all_to_all | solution.py:105
  23.7 55.1 %copy-start.5 = (bf16[192,16,128]{2,0,1:T(8,128)(2,1)}, bf16[192,16,128]{2,0,1:T(8,128)(2,1)S(1)}, u32[]{:S(2)}) copy-start(bf16[192,16,128]{2,0,1:T(8,128)(2,1)S(1)} %all-to-all-done.1) | copy-start | bytes 2359300
  23.7 18.7 %all-to-all-start.2 = ((bf16[192,16,128]{2,0,1:T(8,128)(2,1)}), bf16[192,16,128]{2,0,1:T(8,128)(2,1)S(1)}, u32[]{:S(2)}, u32[]{:S(2)}) async-start(bf16[192,16,128]{2,0,1:T(8,128)(2,1)} %copy_bitcast_fusion.4), calls=%async_computation.2 | async-start | bytes 1572864 | tf_op jit(solution)/shard_map/all_to_all | solution.py:105
  42.4 0.9 copy-start.7
  43.3 27.3 %all-to-all-start = ((bf16[192,16,256]{2,0,1:T(8,128)(2,1)}), bf16[192,16,256]{2,0,1:T(8,128)(2,1)S(1)}, u32[]{:S(2)}, u32[]{:S(2)}) async-start(bf16[192,16,256]{2,0,1:T(8,128)(2,1)} %bitcast.47), calls=%async_computation | async-start | bytes 3145728 | tf_op jit(solution)/shard_map/all_to_all | solution.py:105
  70.6 1.1 copy-start.4
  71.8 39.2 %all-to-all-start.3 = ((bf16[192,16,256]{2,0,1:T(8,128)(2,1)}), bf16[192,16,256]{2,0,1:T(8,128)(2,1)}, u32[]{:S(2)}, u32[]{:S(2)}) async-start(bf16[192,16,256]{2,0,1:T(8,128)(2,1)} %bitcast.46), calls=%async_computation.3 | async-start | bytes 3145728 | tf_op jit(solution)/shard_map/all_to_all | solution.py:105
  78.8 15.4 %copy-start.8 = (bf16[192,16,128]{2,0,1:T(8,128)(2,1)S(1)}, bf16[192,16,128]{2,0,1:T(8,128)(2,1)}, u32[]{:S(2)}) copy-start(bf16[192,16,128]{2,0,1:T(8,128)(2,1)} %copy-done.7) | copy-start | bytes 2359300
  78.9 15.4 %copy-start.6 = (bf16[192,16,128]{2,0,1:T(8,128)(2,1)S(1)}, bf16[192,16,128]{2,0,1:T(8,128)(2,1)}, u32[]{:S(2)}) copy-start(bf16[192,16,128]{2,0,1:T(8,128)(2,1)} %copy-done.5) | copy-start | bytes 2359300
  80.0 14.1 %collective-permute-start = (bf16[1024,256]{1,0:T(8,128)(2,1)S(1)}, bf16[1024,256]{1,0:T(8,128)(2,1)S(1)}, u32[]{:S(2)}, u32[]{:S(2)}) collective-permute-start(bf16[1024,256]{1,0:T(8,128)(2,1)S(1)} %pad_maximum_fusion.4), channel_id=1, source_target_pairs={{0,16},{16,32},{32,48},{48,64},{64,80},{80,96},{96,112},{1,17},{17... | collective-permute-start | bytes 1572872 | tf_op jit(solution)/shard_map/ppermute | solution.py:100
  94.2 16.8 %copy-start.3 = (s32[16]{0:T(128)S(1)}, s32[16]{0:T(128)}, u32[]{:S(2)}) copy-start(s32[16]{0:T(128)} %len_ref.1) | copy-start | bytes 196
  148.6 15.2 %copy-start.1 = (bf16[4096,128]{1,0:T(8,128)(2,1)}, bf16[4096,128]{1,0:T(8,128)(2,1)S(1)}, u32[]{:S(2)}) copy-start(bf16[4096,128]{1,0:T(8,128)(2,1)S(1)} %get-tuple-element.7) | copy-start | bytes 3145732
  148.7 15.0 %collective-permute-start.1 = (bf16[1024,256]{1,0:T(8,128)(2,1)S(1)}, bf16[1024,256]{1,0:T(8,128)(2,1)S(1)}, u32[]{:S(2)}, u32[]{:S(2)}) collective-permute-start(bf16[1024,256]{1,0:T(8,128)(2,1)S(1)} %pad_maximum_fusion.5), channel_id=1, source_target_pairs={{16,0},{32,16},{48,32},{64,48},{80,64},{96,80},{112,96},{17,1},{33... | collective-permute-start | bytes 1572872 | tf_op jit(solution)/shard_map/ppermute | solution.py:100
  163.9 6.5 %copy-start.2 = (bf16[4096,128]{1,0:T(8,128)(2,1)S(1)}, bf16[4096,128]{1,0:T(8,128)(2,1)}, u32[]{:S(2)}) copy-start(bf16[4096,128]{1,0:T(8,128)(2,1)} %copy-done.1) | copy-start | bytes 3145732
  164.8 18.0 %all-to-all-start.6 = ((bf16[16,192,128]{2,1,0:T(8,128)(2,1)}), bf16[16,192,128]{2,1,0:T(8,128)(2,1)S(1)}, u32[]{:S(2)}, u32[]{:S(2)}) async-start(bf16[16,192,128]{2,1,0:T(8,128)(2,1)} %bitcast.13), calls=%async_computation.6 | async-start | bytes 1572864 | tf_op jit(solution)/shard_map/all_to_all | solution.py:108
  201.4 26.7 %all-to-all-start.4 = ((bf16[16,192,256]{2,1,0:T(8,128)(2,1)}), bf16[16,192,256]{2,1,0:T(8,128)(2,1)S(1)}, u32[]{:S(2)}, u32[]{:S(2)}) async-start(bf16[16,192,256]{2,1,0:T(8,128)(2,1)} %bitcast.9), calls=%async_computation.4 | async-start | bytes 3145728 | tf_op jit(solution)/shard_map/all_to_all | solution.py:108
  207.3 1.4 copy-start.9

commit v2 on v1

v2 whole, which is shorter than its diff:
```python
import functools
import jax
import jax.numpy as jnp
from jax import lax
from jax.experimental import pallas as pl
from jax.experimental.pallas import tpu as pltpu
from jax.sharding import PartitionSpec as P

HD = 128
WINDOW = 1024
BQ = 256
BK = 256
NT=(WINDOW+BQ)//BK
SCALE=HD**-0.5
C2=SCALE*1.4426950408889634
NEG=-1e30
f32 = jnp.float32
bf16 = jnp.bfloat16
NTK=(((1,),(1,)),((),()))
NN=(((1,),(0,)),((),()))

def block(b, base, len_ref, q, do, k_ref, v_ref, kt_ref, dk_ref, dv_ref, s_scr, p_scr):
    first = base + b*BQ - WINDOW
    qi = lax.broadcasted_iota(jnp.int32,(1,BQ),1)
    gpos = first + WINDOW + qi
    end = jnp.int32(0)
    start = jnp.zeros((1,BQ),jnp.int32)
    for d in range(16):
        end = end + len_ref[d]
        start = jnp.where(gpos >= end, end, start)
    lo = jnp.maximum(qi+1, start-first)
    ki = lax.broadcasted_iota(jnp.int32,(BK,BQ),0)
    m = None
    for t in range(NT):
        r = pl.multiple_of(b*BQ + t*BK, BK)
        s = lax.dot_general(k_ref[pl.ds(r,BK),:], q, NTK, preferred_element_type=f32)
        ok = ki >= lo - t*BK
        if t==NT-1:
            ok = ok & (ki <= lax.broadcasted_iota(jnp.int32,(BK,BQ),1))
        s = jnp.where(ok, s, NEG)
        s_scr[t] = s
        mt = jnp.max(s.reshape(BK//8,8,BQ),axis=0)
        m = mt if m is None else jnp.maximum(m,mt)
    m = jnp.max(m,axis=0,keepdims=True)
    l = jnp.zeros((8,BQ),f32); dd = jnp.zeros((8,BQ),f32)
    for t in range(NT):
        r = pl.multiple_of(b*BQ + t*BK, BK)
        p = jnp.exp2((s_scr[t]-m)*C2)
        s_scr[t] = p
        dp = lax.dot_general(v_ref[pl.ds(r,BK),:], do, NTK, preferred_element_type=f32)
        p_scr[t] = dp
        l = l + jnp.sum(p.reshape(BK//8,8,BQ),axis=0)
        dd = dd + jnp.sum((p*dp).reshape(BK//8,8,BQ),axis=0)
    l = jnp.sum(l,axis=0,keepdims=True); dd = jnp.sum(dd,axis=0,keepdims=True)
    inv = 1.0/l
    dd = dd*inv
    dqt = None
    for t in range(NT):
        r = pl.multiple_of(b*BQ + t*BK, BK)
        w = s_scr[t]*inv
        ds = (w*(p_scr[t]-dd)).astype(bf16)
        dv_ref[pl.ds(r,BK),:] += lax.dot_general(w.astype(bf16), do, NN, preferred_element_type=f32)
        dk_ref[pl.ds(r,BK),:] += lax.dot_general(ds, q, NN, preferred_element_type=f32)
        x = lax.dot_general(kt_ref[:,pl.ds(r,BK)], ds, NN, preferred_element_type=f32)
        dqt = x if dqt is None else dqt + x
    return (dqt*SCALE).T


def exchange_kernel(
    heads, groups,
    len_ref, q_hbm, k_hbm, v_hbm, do_hbm,
    dq_hbm, dk_hbm, dv_hbm,
    qb, dob, kx, vx, kt, dk, dv, dqo, dko, dvo, rk, rv, s_scr, p_scr,
    in_send, in_recv, out_send, out_recv, halo_send, halo_recv, rim_send, rim_recv,
):
    rows = q_hbm.shape[0]
    group = heads * rows
    tiles = group // BQ
    rim_tiles = WINDOW // BQ
    per = q_hbm.shape[1] // k_hbm.shape[1]
    me = lax.axis_index("head")
    seq = lax.axis_index("seq")
    base = seq * group
    MESH = pl.DeviceIdType.MESH

    def peer(t):
        return lax.rem(me + t, heads)

    barrier = pltpu.get_barrier_semaphore()

    def greet(t, c):
        pl.semaphore_signal(barrier, inc=1, device_id=(seq, peer(t)), device_id_type=MESH)
        return c

    lax.fori_loop(1, heads, greet, 0)

    for by in (1, groups - 1):
        near = lax.rem(seq + by, groups)
        pl.semaphore_signal(barrier, inc=1, device_id=(near, me), device_id_type=MESH)

    def source(kind, p):
        if kind == 0:
            return k_hbm.at[:, pl.ds(pl.multiple_of(p * HD, HD), HD)]
        if kind == 1:
            return v_hbm.at[:, pl.ds(pl.multiple_of(p * HD, HD), HD)]
        h = (kind - 2) // 2
        ref = q_hbm if kind % 2 == 0 else do_hbm
        return ref.at[:, pl.ds(pl.multiple_of((p * per + h) * HD, HD), HD)]

    def target(kind, j):
        own = pl.ds(pl.multiple_of(j * rows, 64), rows)
        if kind < 2:
            ref = kx if kind == 0 else vx
            return ref.at[pl.ds(pl.multiple_of(WINDOW + j * rows, 64), rows), :]
        ref = qb if kind % 2 == 0 else dob
        return ref.at[(kind - 2) // 2, own, :]

    kinds = 2 + 2 * per

    def in_copy(kind, t):
        p = peer(t)
        return pltpu.make_async_remote_copy(
            src_ref=source(kind, p), dst_ref=target(kind, me),
            send_sem=in_send.at[kind, t], recv_sem=in_recv.at[kind, me],
            device_id=(seq, p), device_id_type=MESH,
        )

    def own_copy(kind):
        return pltpu.make_async_copy(source(kind, me), target(kind, me), in_recv.at[kind, me])

    def arrived(kind, j):
        pltpu.make_async_copy(target(kind, j), target(kind, j), in_recv.at[kind, j]).wait()

    for kind in range(kinds):
        own_copy(kind).start()

    def clear(i, c):
        r = pl.multiple_of(i * BK, BK)
        dk[pl.ds(r, BK), :] = jnp.zeros((BK, HD), f32)
        dv[pl.ds(r, BK), :] = jnp.zeros((BK, HD), f32)
        return c

    lax.fori_loop(0, (WINDOW + group) // BK, clear, 0)

    pl.semaphore_wait(barrier, heads + 1)

    for first in range(0, kinds, 2):
        def send(t, c):
            in_copy(first, t).start()
            in_copy(first + 1, t).start()
            return c

        lax.fori_loop(1, heads, send, 0)

    def halo(i):
        ref = kx if i == 0 else vx
        return pltpu.make_async_remote_copy(
            src_ref=ref.at[pl.ds(group, WINDOW), :], dst_ref=ref.at[pl.ds(0, WINDOW), :],
            send_sem=halo_send.at[i], recv_sem=halo_recv.at[i],
            device_id=(seq + 1, me), device_id_type=MESH,
        )

    def kv_wait(j, c):
        arrived(0, j)
        arrived(1, j)
        return c

    late = (group - WINDOW) // rows
    lax.fori_loop(late, heads, kv_wait, 0)

    @pl.when(seq < groups - 1)
    def _():
        halo(0).start()
        halo(1).start()

    lax.fori_loop(0, late, kv_wait, 0)

    def turn(i, c):
        r = pl.multiple_of(i * BK, BK)
        kt[:, pl.ds(r, BK)] = kx[pl.ds(r, BK), :].T
        return c

    lax.fori_loop(WINDOW // BK, (WINDOW + group) // BK, turn, 0)

    @pl.when(seq == 0)
    def _():
        kx[pl.ds(0, WINDOW), :] = jnp.zeros((WINDOW, HD), bf16)
        vx[pl.ds(0, WINDOW), :] = jnp.zeros((WINDOW, HD), bf16)

    @pl.when(seq > 0)
    def _():
        for i, ref in enumerate((kx, vx)):
            own = ref.at[pl.ds(0, WINDOW), :]
            pltpu.make_async_copy(own, own, halo_recv.at[i]).wait()

    lax.fori_loop(0, WINDOW // BK, turn, 0)

    def out_parts(kind, h, j):
        own = pl.ds(pl.multiple_of(j * rows, 64), rows)
        ext = pl.ds(pl.multiple_of(WINDOW + j * rows, 64), rows)
        if kind == 0:
            col = pl.ds(pl.multiple_of((me * per + h) * HD, HD), HD)
            return dqo.at[h, own, :], dq_hbm.at[:, col], h
        col = pl.ds(pl.multiple_of(me * HD, HD), HD)
        if kind == 1:
            return dko.at[ext, :], dk_hbm.at[:, col], per
        return dvo.at[ext, :], dv_hbm.at[:, col], per + 1

    def out_copy(kind, h, j):
        src, dst, row = out_parts(kind, h, j)
        return pltpu.make_async_remote_copy(
            src_ref=src, dst_ref=dst,
            send_sem=out_send.at[row, j], recv_sem=out_recv.at[row, me],
            device_id=(seq, j), device_id_type=MESH,
        )

    def out_own(kind, h):
        src, dst, row = out_parts(kind, h, me)
        return pltpu.make_async_copy(src, dst, out_recv.at[row, me])

    def deliver(kind, h, lo, hi):
        def one(j, c):
            @pl.when(j != me)
            def _():
                out_copy(kind, h, j).start()

            @pl.when(j == me)
            def _():
                out_own(kind, h).start()

            return c

        lax.fori_loop(lo, hi, one, 0)

    def rim(i, b):
        src = (dko, dvo)[i].at[pl.ds(pl.multiple_of(b * BQ, BQ), BQ), :]
        dst = (rk, rv)[i].at[pl.ds(pl.multiple_of(b * BQ, BQ), BQ), :]
        return pltpu.make_async_remote_copy(
            src_ref=src, dst_ref=dst,
            send_sem=rim_send.at[i, b], recv_sem=rim_recv.at[i, b],
            device_id=(seq - 1, me), device_id_type=MESH,
        )

    def step(it, c):
        h = it // tiles
        b = lax.rem(it, tiles)
        r = pl.multiple_of(b * BQ, BQ)

        def wait_rows(j, c):
            own = pl.ds(pl.multiple_of(j * rows, 64), rows)
            for i, ref in enumerate((qb, dob)):
                view = ref.at[h, own, :]
                pltpu.make_async_copy(view, view, in_recv.at[2 + 2 * h + i, j]).wait()
            return c

        lax.fori_loop((BQ * b + rows - 1) // rows, (BQ * b + BQ - 1) // rows + 1, wait_rows, 0)
        q = qb[h, pl.ds(r, BQ), :]
        do = dob[h, pl.ds(r, BQ), :]
        grad = block(b, base, len_ref, q, do, kx, vx, kt, dk, dv, s_scr, p_scr)
        dqo[h, pl.ds(r, BQ), :] = grad.astype(bf16)
        deliver(0, h, BQ * b // rows, BQ * (b + 1) // rows)

        @pl.when(h == per - 1)
        def _():
            dko[pl.ds(r, BQ), :] = (dk[pl.ds(r, BQ), :] * SCALE).astype(bf16)
            dvo[pl.ds(r, BQ), :] = dv[pl.ds(r, BQ), :].astype(bf16)

            @pl.when((b < rim_tiles) & (seq > 0))
            def _():
                rim(0, b).start()
                rim(1, b).start()

            @pl.when(b >= rim_tiles)
            def _():
                o = b - rim_tiles
                for kind in (1, 2):
                    deliver(kind, 0, BQ * o // rows, BQ * (o + 1) // rows)

        return c

    lax.fori_loop(0, per * tiles, step, 0)

    def last(i, c):
        r = pl.multiple_of(group + i * BQ, BQ)
        o = pl.multiple_of(i * BQ, BQ)

        @pl.when(seq < groups - 1)
        def _():
            for n, ref in enumerate((rk, rv)):
                view = ref.at[pl.ds(o, BQ), :]
                pltpu.make_async_copy(view, view, rim_recv.at[n, i]).wait()
            dko[pl.ds(r, BQ), :] = (dk[pl.ds(r, BQ), :] * SCALE + rk[pl.ds(o, BQ), :].astype(f32)).astype(bf16)
            dvo[pl.ds(r, BQ), :] = (dv[pl.ds(r, BQ), :] + rv[pl.ds(o, BQ), :].astype(f32)).astype(bf16)

        @pl.when(seq == groups - 1)
        def _():
            dko[pl.ds(r, BQ), :] = (dk[pl.ds(r, BQ), :] * SCALE).astype(bf16)
            dvo[pl.ds(r, BQ), :] = dv[pl.ds(r, BQ), :].astype(bf16)

        b = tiles - rim_tiles + i
        for kind in (1, 2):
            deliver(kind, 0, BQ * b // rows, BQ * (b + 1) // rows)
        return c

    lax.fori_loop(0, rim_tiles, last, 0)

    def finish(t, c):
        p = peer(t)
        for kind in range(kinds):
            in_copy(kind, t).wait_send()
        for h in range(per):
            out_copy(0, h, p).wait_send()
        out_copy(1, 0, p).wait_send()
        out_copy(2, 0, p).wait_send()
        return c

    lax.fori_loop(1, heads, finish, 0)

    def landed(j, c):
        for row in range(per + 2):
            ref = dq_hbm if row < per else (dk_hbm, dv_hbm)[row - per]
            col = (j * per + row) * HD if row < per else j * HD
            view = ref.at[:, pl.ds(pl.multiple_of(col, HD), HD)]
            pltpu.make_async_copy(view, view, out_recv.at[row, j]).wait()
        return c

    lax.fori_loop(0, heads, landed, 0)

    @pl.when(seq < groups - 1)
    def _():
        halo(0).wait_send()
        halo(1).wait_send()

    @pl.when(seq > 0)
    def _():
        for b in range(rim_tiles):
            rim(0, b).wait_send()
            rim(1, b).wait_send()


def local(queries, keys, values, grad_out, doc_lengths):
    heads, groups = lax.axis_size("head"), lax.axis_size("seq")
    rows = queries.shape[0]
    group = heads * rows
    ext = group + WINDOW
    per = queries.shape[1] // keys.shape[1]
    hbm = pl.BlockSpec(memory_space=pl.ANY)
    dma = pltpu.SemaphoreType.DMA
    return pl.pallas_call(
        functools.partial(exchange_kernel, heads, groups),
        out_shape=(
            jax.ShapeDtypeStruct(queries.shape, bf16),
            jax.ShapeDtypeStruct(keys.shape, bf16),
            jax.ShapeDtypeStruct(values.shape, bf16),
        ),
        in_specs=[pl.BlockSpec(memory_space=pltpu.SMEM), hbm, hbm, hbm, hbm],
        out_specs=(hbm, hbm, hbm),
        scratch_shapes=[
            pltpu.VMEM((per, group, HD), bf16),
            pltpu.VMEM((per, group, HD), bf16),
            pltpu.VMEM((ext, HD), bf16),
            pltpu.VMEM((ext, HD), bf16),
            pltpu.VMEM((HD, ext), bf16),
            pltpu.VMEM((ext, HD), f32),
            pltpu.VMEM((ext, HD), f32),
            pltpu.VMEM((per, group, HD), bf16),
            pltpu.VMEM((ext, HD), bf16),
            pltpu.VMEM((ext, HD), bf16),
            pltpu.VMEM((WINDOW, HD), bf16),
            pltpu.VMEM((WINDOW, HD), bf16),
            pltpu.VMEM((NT, BK, BQ), f32),
            pltpu.VMEM((NT, BK, BQ), f32),
            dma((2 + 2 * per, heads)),
            dma((2 + 2 * per, heads)),
            dma((2 + per, heads)),
            dma((2 + per, heads)),
            dma((2,)),
            dma((2,)),
            dma((2, WINDOW // BQ)),
            dma((2, WINDOW // BQ)),
        ],
        compiler_params=pltpu.CompilerParams(
            collective_id=0, has_side_effects=True, vmem_limit_bytes=48 << 20
        ),
    )(doc_lengths, queries, keys, values, grad_out)


def solution(mesh):
    rows = P(("seq", "head"), None)
    return jax.shard_map(
        local,
        mesh=mesh,
        in_specs=(rows, rows, rows, rows, P()),
        out_specs=(rows, rows, rows),
        check_vma=False,
    )
```

time: 233 us -> 126 us (0.54)
  the two profiles are of different devices: /device:TPU:7 before, /device:TPU:127 now
where the time goes in v2:
time: 126 us
  Pallas kernels  119 us (94%)
  local copies, waits for them, and re-layouts  5.82 us (5%)
    pallas_call x1, Pallas kernels, local(): pl.pallas_call(functools.partial(exchange_kernel, heads, groups), out_sha...  119 us
    unnamed x9, local copies, waits for them, and re-layouts  5.82 us

profile of v2, /device:TPU:127, one launch (start us, length us, event | category | flops | bytes accessed | tf_op | source)
XLA Modules:
  0.0 125.6 jit_solution(2972167907603374806)
XLA Ops:
  0.6 0.0 copy-start
  0.6 1.1 copy-done
  1.8 0.0 copy-start.1
  1.8 1.1 copy-done.1
  2.9 0.0 copy-start.2
  2.9 0.7 copy-done.2
  3.6 119.1 %shard_map.76 = (bf16[192,4096]{1,0:T(8,128)(2,1)S(1)}, bf16[192,2048]{1,0:T(8,128)(2,1)S(1)}, bf16[192,2048]{1,0:T(8,128)(2,1)S(1)}) custom-call(s32[16]{0:T(128)S(1)} %copy-done.2, bf16[192,4096]{1,0:T(8,128)(2,1)} %q_hbm.1, bf16[192,2048]{1,0:T(8,128)(2,1)S(1)} %copy-done, bf16[192,2048]{1,0:T(8,128)(2,1)S(1)} %copy-done.1, bf16[192,4096]{1,0:T(8,128)(2,1)} %do_hbm.1), custom_call_target="tpu_custom_call" | custom-call | tf_op jit(solution)/shard_map/pallas_call | solution.py:349
  122.7 1.1 copy.11
  123.8 0.9 copy.12
  124.7 0.9 copy.13
Async XLA Ops:
  0.6 1.1 copy-start
  1.8 1.1 copy-start.1
  2.9 0.7 copy-start.2

commit v3 on v2

v3 whole, which is shorter than its diff:
```python
import functools

import jax
import jax.numpy as jnp
from jax import lax
from jax.experimental import pallas as pl
from jax.experimental.pallas import tpu as pltpu
from jax.sharding import PartitionSpec as P

HD = 128
WINDOW = 1024
BQ = 256
BK = 256
NT=(WINDOW+BQ)//BK
SCALE=HD**-0.5
C2=SCALE*1.4426950408889634
NEG=-1e30
f32 = jnp.float32
bf16 = jnp.bfloat16
NTK=(((1,),(1,)),((),()))
NN=(((1,),(0,)),((),()))
def block(b, base, len_ref, qs, dos, k_ref, v_ref, kt_ref, dk_ref, dv_ref, s_scr, p_scr):
    per=len(qs)
    first = base + b*BQ - WINDOW
    qi = lax.broadcasted_iota(jnp.int32,(1,BQ),1)
    gpos = first + WINDOW + qi
    end = jnp.int32(0)
    start = jnp.zeros((1,BQ),jnp.int32)
    for d in range(16):
        end = end + len_ref[d]
        start = jnp.where(gpos >= end, end, start)
    lo = jnp.maximum(qi+1, start-first)
    ki = lax.broadcasted_iota(jnp.int32,(BK,BQ),0)
    rows=[pl.ds(pl.multiple_of(b*BQ + t*BK, BK),BK) for t in range(NT)]
    stats=[]
    for h in range(per):
        q,do=qs[h],dos[h]
        m = None
        for t in range(NT):
            s = lax.dot_general(k_ref[rows[t],:], q, NTK, preferred_element_type=f32)
            ok = ki >= lo - t*BK
            if t==NT-1:
                ok = ok & (ki <= lax.broadcasted_iota(jnp.int32,(BK,BQ),1))
            s = jnp.where(ok, s, NEG)
            s_scr[h,t] = s
            mt = jnp.max(s.reshape(BK//8,8,BQ),axis=0)
            m = mt if m is None else jnp.maximum(m,mt)
        m = jnp.max(m,axis=0,keepdims=True)
        l = jnp.zeros((8,BQ),f32); dd = jnp.zeros((8,BQ),f32)
        for t in range(NT):
            p = jnp.exp2((s_scr[h,t]-m)*C2)
            s_scr[h,t] = p
            dp = lax.dot_general(v_ref[rows[t],:], do, NTK, preferred_element_type=f32)
            p_scr[h,t] = dp
            l = l + jnp.sum(p.reshape(BK//8,8,BQ),axis=0)
            dd = dd + jnp.sum((p*dp).reshape(BK//8,8,BQ),axis=0)
        l = jnp.sum(l,axis=0,keepdims=True); dd = jnp.sum(dd,axis=0,keepdims=True)
        inv = 1.0/l
        stats.append((inv,dd*inv))
    dqt = [None]*per
    q_all=jnp.concatenate(qs,axis=0); do_all=jnp.concatenate(dos,axis=0)
    for t in range(NT):
        ws=[];dss=[]
        for h in range(per):
            inv,dd=stats[h]
            w = s_scr[h,t]*inv
            ds = (w*(p_scr[h,t]-dd)).astype(bf16)
            ws.append(w.astype(bf16)); dss.append(ds)
            x = lax.dot_general(kt_ref[:,rows[t]], ds, NN, preferred_element_type=f32)
            dqt[h] = x if dqt[h] is None else dqt[h] + x
        dv_ref[rows[t],:] += lax.dot_general(jnp.concatenate(ws,axis=1), do_all, NN, preferred_element_type=f32)
        dk_ref[rows[t],:] += lax.dot_general(jnp.concatenate(dss,axis=1), q_all, NN, preferred_element_type=f32)
    return [(x*SCALE).T for x in dqt]


def exchange_kernel(
    heads, groups,
    len_ref, q_hbm, k_hbm, v_hbm, do_hbm,
    dq_hbm, dk_hbm, dv_hbm,
    qb, dob, kx, vx, kt, dk, dv, dqo, dko, dvo, rk, rv, s_scr, p_scr,
    in_send, in_recv, out_send, out_recv, halo_send, halo_recv, rim_send, rim_recv,
):
    rows = q_hbm.shape[0]
    group = heads * rows
    tiles = group // BQ
    per = q_hbm.shape[1] // k_hbm.shape[1]
    wide = per * HD
    me = lax.axis_index("head")
    seq = lax.axis_index("seq")
    base = seq * group
    MESH = pl.DeviceIdType.MESH

    quads = heads // 4
    per_quad = tiles // quads
    mine, place = me // 4, lax.rem(me, 4)
    start = lax.rem(mine + 1 + place, quads)

    def quad_at(n):
        return lax.rem(start + n, quads)

    def receiver(i):
        to = lax.rem(place + lax.rem(i, 4), 4)
        return lax.rem(mine + 3 * quads - 1 - to - i // 4, quads) * 4 + to

    def peer(t):
        return lax.rem(me + t, heads)

    half = groups // 2

    def traded(p, yes):
        return p + lax.rem(p, 2) * yes * (2 - 4 * lax.rem(p // 2, 2))

    def head_of(p):
        return traded(p, seq // half)

    after = lax.rem(seq + 1, groups)
    before = lax.rem(seq + groups - 1, groups)
    next_id = (after, traded(me, lax.rem(seq // half + after // half, 2)))
    prev_id = (before, traded(me, lax.rem(seq // half + before // half, 2)))

    barrier = pltpu.get_barrier_semaphore()

    def greet(t, c):
        pl.semaphore_signal(barrier, inc=1, device_id=(seq, peer(t)), device_id_type=MESH)
        return c

    lax.fori_loop(1, heads, greet, 0)
    for near in (next_id, prev_id):
        pl.semaphore_signal(barrier, inc=1, device_id=near, device_id_type=MESH)

    sources = (k_hbm, v_hbm, q_hbm, do_hbm)
    targets = (kx, vx, qb, dob)
    widths = (HD, HD, wide, wide)

    def target(kind, j):
        first = j * rows + (WINDOW if kind < 2 else 0)
        return targets[kind].at[pl.ds(pl.multiple_of(first, 64), rows), :]

    def source(kind, p):
        w = widths[kind]
        return sources[kind].at[:, pl.ds(pl.multiple_of(head_of(p) * w, w), w)]

    def in_copy(kind, p):
        return pltpu.make_async_remote_copy(
            src_ref=source(kind, p), dst_ref=target(kind, me),
            send_sem=in_send.at[kind, p], recv_sem=in_recv.at[kind, me],
            device_id=(seq, p), device_id_type=MESH,
        )

    def arrived(kind, j):
        pltpu.make_async_copy(target(kind, j), target(kind, j), in_recv.at[kind, j]).wait()

    for kind in range(4):
        pltpu.make_async_copy(source(kind, me), target(kind, me), in_recv.at[kind, me]).start()

    def clear(i, c):
        r = pl.multiple_of(i * BK, BK)
        dk[pl.ds(r, BK), :] = jnp.zeros((BK, HD), f32)
        dv[pl.ds(r, BK), :] = jnp.zeros((BK, HD), f32)
        return c

    lax.fori_loop(0, (WINDOW + group) // BK, clear, 0)

    pl.semaphore_wait(barrier, heads + 1)

    for first in (0, 2):
        def send(i, c):
            p = receiver(i)

            @pl.when(p != me)
            def _():
                in_copy(first, p).start()
                in_copy(first + 1, p).start()

            return c

        lax.fori_loop(0, heads, send, 0)

    def halo(i):
        ref = (kx, vx)[i]
        return pltpu.make_async_remote_copy(
            src_ref=ref.at[pl.ds(group, WINDOW), :], dst_ref=ref.at[pl.ds(0, WINDOW), :],
            send_sem=halo_send.at[i], recv_sem=halo_recv.at[i],
            device_id=next_id, device_id_type=MESH,
        )

    def kv_wait(j, c):
        arrived(0, j)
        arrived(1, j)
        return c

    late = (group - WINDOW) // rows
    lax.fori_loop(late, heads, kv_wait, 0)

    @pl.when(seq < groups - 1)
    def _():
        halo(0).start()
        halo(1).start()

    lax.fori_loop(0, late, kv_wait, 0)

    def turn(i, c):
        r = pl.multiple_of(i * BK, BK)
        kt[:, pl.ds(r, BK)] = kx[pl.ds(r, BK), :].T
        return c

    lax.fori_loop(WINDOW // BK, (WINDOW + group) // BK, turn, 0)

    def halo_wait():
        @pl.when(seq == 0)
        def _():
            kx[pl.ds(0, WINDOW), :] = jnp.zeros((WINDOW, HD), bf16)
            vx[pl.ds(0, WINDOW), :] = jnp.zeros((WINDOW, HD), bf16)

        @pl.when(seq > 0)
        def _():
            for i, ref in enumerate((kx, vx)):
                own = ref.at[pl.ds(0, WINDOW), :]
                pltpu.make_async_copy(own, own, halo_recv.at[i]).wait()

        lax.fori_loop(0, WINDOW // BK, turn, 0)

    staged = (dqo, dko, dvo)
    results = (dq_hbm, dk_hbm, dv_hbm)

    def out_parts(kind, j):
        first = j * rows + (WINDOW if kind else 0)
        w = HD if kind else wide
        src = staged[kind].at[pl.ds(pl.multiple_of(first, 64), rows), :]
        return src, results[kind].at[:, pl.ds(pl.multiple_of(head_of(me) * w, w), w)]

    def out_copy(kind, j):
        src, dst = out_parts(kind, j)
        return pltpu.make_async_remote_copy(
            src_ref=src, dst_ref=dst,
            send_sem=out_send.at[kind, j], recv_sem=out_recv.at[kind, me],
            device_id=(seq, j), device_id_type=MESH,
        )

    def deliver(kinds, lo, count):
        def one(i, c):
            j = lo + lax.rem(i + place, count)
            for kind in kinds:
                @pl.when(j != me)
                def _():
                    out_copy(kind, j).start()

                @pl.when(j == me)
                def _():
                    src, dst = out_parts(kind, me)
                    pltpu.make_async_copy(src, dst, out_recv.at[kind, me]).start()

            return c

        lax.fori_loop(0, count, one, 0)

    def rim(i):
        return pltpu.make_async_remote_copy(
            src_ref=(dko, dvo)[i].at[pl.ds(0, WINDOW), :], dst_ref=(rk, rv)[i],
            send_sem=rim_send.at[i], recv_sem=rim_recv.at[i],
            device_id=prev_id, device_id_type=MESH,
        )

    def stage(lo, count):
        def one(i, c):
            r = pl.multiple_of(lo + i * 128, 128)
            dko[pl.ds(r, 128), :] = (dk[pl.ds(r, 128), :] * SCALE).astype(bf16)
            dvo[pl.ds(r, 128), :] = dv[pl.ds(r, 128), :].astype(bf16)
            return c

        lax.fori_loop(0, count // 128, one, 0)

    def at_stage(y, over):
        off = lax.rem(y - start + 2 * quads, quads)
        return jnp.where(off + over < quads, off + over, quads - 1)

    def step(n, c):
        quad = quad_at(n)

        def rows_wait(j, c):
            arrived(2, j)
            arrived(3, j)
            return c

        lax.fori_loop(quad * 4, quad * 4 + 4, rows_wait, 0)

        def tile(i, c):
            b = quad * per_quad + lax.rem(i + 1, per_quad)
            first_use = jnp.where(start == 1, per_quad, 1)

            @pl.when(b == first_use)
            def _():
                halo_wait()

            r = pl.multiple_of(b * BQ, BQ)
            qs = [qb[pl.ds(r, BQ), h * HD : (h + 1) * HD] for h in range(per)]
            dos = [dob[pl.ds(r, BQ), h * HD : (h + 1) * HD] for h in range(per)]
            grads = block(b, base, len_ref, qs, dos, kx, vx, kt, dk, dv, s_scr, p_scr)
            for h in range(per):
                dqo[pl.ds(r, BQ), h * HD : (h + 1) * HD] = grads[h].astype(bf16)
            return c

        lax.fori_loop(0, per_quad, tile, 0)
        deliver((0,), quad * 4, 4)

        @pl.when(n == at_stage(0, 1))
        def _():
            @pl.when(seq > 0)
            def _():
                stage(0, WINDOW)
                rim(0).start()
                rim(1).start()

        for y, count in ((0, 4), (1, 4), (2, late - 8)):
            @pl.when(n == at_stage(y, min(2, quads - 1 - y)))
            def _():
                stage(WINDOW + y * 4 * rows, count * rows)
                deliver((1, 2), y * 4, count)

        return c

    lax.fori_loop(0, quads, step, 0)

    @pl.when(seq < groups - 1)
    def _():
        for i, ref in enumerate((rk, rv)):
            pltpu.make_async_copy(ref, ref, rim_recv.at[i]).wait()

    def last(i, c):
        r = pl.multiple_of(group + i * 128, 128)
        o = pl.multiple_of(i * 128, 128)

        @pl.when(seq < groups - 1)
        def _():
            dk[pl.ds(r, 128), :] += rk[pl.ds(o, 128), :].astype(f32) * (1.0 / SCALE)
            dv[pl.ds(r, 128), :] += rv[pl.ds(o, 128), :].astype(f32)

        return c

    lax.fori_loop(0, WINDOW // 128, last, 0)
    stage(WINDOW + late * rows, (heads - late) * rows)
    deliver((1, 2), late, heads - late)

    def finish(t, c):
        p = peer(t)
        for kind in range(4):
            in_copy(kind, p).wait_send()
        for kind in range(3):
            out_copy(kind, p).wait_send()
        return c

    lax.fori_loop(1, heads, finish, 0)

    def landed(j, c):
        for kind in range(3):
            w = HD if kind else wide
            view = results[kind].at[:, pl.ds(pl.multiple_of(head_of(j) * w, w), w)]
            pltpu.make_async_copy(view, view, out_recv.at[kind, j]).wait()
        return c

    lax.fori_loop(0, heads, landed, 0)

    @pl.when(seq < groups - 1)
    def _():
        halo(0).wait_send()
        halo(1).wait_send()

    @pl.when(seq > 0)
    def _():
        rim(0).wait_send()
        rim(1).wait_send()


def local(queries, keys, values, grad_out, doc_lengths):
    heads, groups = lax.axis_size("head"), lax.axis_size("seq")
    rows = queries.shape[0]
    group = heads * rows
    ext = group + WINDOW
    per = queries.shape[1] // keys.shape[1]
    hbm = pl.BlockSpec(memory_space=pl.ANY)
    dma = pltpu.SemaphoreType.DMA
    return pl.pallas_call(
        functools.partial(exchange_kernel, heads, groups),
        out_shape=(
            jax.ShapeDtypeStruct(queries.shape, bf16),
            jax.ShapeDtypeStruct(keys.shape, bf16),
            jax.ShapeDtypeStruct(values.shape, bf16),
        ),
        in_specs=[pl.BlockSpec(memory_space=pltpu.SMEM), hbm, hbm, hbm, hbm],
        out_specs=(hbm, hbm, hbm),
        scratch_shapes=[
            pltpu.VMEM((group, per * HD), bf16),
            pltpu.VMEM((group, per * HD), bf16),
            pltpu.VMEM((ext, HD), bf16),
            pltpu.VMEM((ext, HD), bf16),
            pltpu.VMEM((HD, ext), bf16),
            pltpu.VMEM((ext, HD), f32),
            pltpu.VMEM((ext, HD), f32),
            pltpu.VMEM((group, per * HD), bf16),
            pltpu.VMEM((ext, HD), bf16),
            pltpu.VMEM((ext, HD), bf16),
            pltpu.VMEM((WINDOW, HD), bf16),
            pltpu.VMEM((WINDOW, HD), bf16),
            pltpu.VMEM((per, NT, BK, BQ), f32),
            pltpu.VMEM((per, NT, BK, BQ), f32),
            dma((4, heads)),
            dma((4, heads)),
            dma((3, heads)),
            dma((3, heads)),
            dma((2,)),
            dma((2,)),
            dma((2,)),
            dma((2,)),
        ],
        compiler_params=pltpu.CompilerParams(
            collective_id=0, has_side_effects=True, vmem_limit_bytes=60 << 20
        ),
    )(doc_lengths, queries, keys, values, grad_out)


def solution(mesh):
    rows = P(("seq", "head"), None)
    return jax.shard_map(
        local,
        mesh=mesh,
        in_specs=(rows, rows, rows, rows, P()),
        out_specs=(rows, rows, rows),
        check_vma=False,
    )
```

time: 126 us -> 126 us (level)
  the two profiles are of different devices: /device:TPU:127 before, /device:TPU:1 now
where the time goes in v3:
time: 126 us; the launch traced here: 125 us
  Pallas kernels  120 us (95%)
  local copies, waits for them, and re-layouts  5.07 us (4%)
    pallas_call x1, Pallas kernels, local(): pl.pallas_call(functools.partial(exchange_kernel, heads, groups), out_sha...  120 us
    unnamed x7, local copies, waits for them, and re-layouts  5.07 us

profile of v3, /device:TPU:1, one launch (start us, length us, event | category | flops | bytes accessed | tf_op | source)
XLA Modules:
  0.0 125.5 jit_solution(13183220218376300860)
XLA Ops:
  0.6 119.8 %shard_map.76 = (bf16[192,4096]{1,0:T(8,128)(2,1)}, bf16[192,2048]{1,0:T(8,128)(2,1)}, bf16[192,2048]{1,0:T(8,128)(2,1)}) custom-call(s32[16]{0:T(128)} %len_ref.1, bf16[192,4096]{1,0:T(8,128)(2,1)} %q_hbm.1, bf16[192,2048]{1,0:T(8,128)(2,1)} %k_hbm.1, bf16[192,2048]{1,0:T(8,128)(2,1)} %v_hbm.1, bf16[192,4096]{1,0:T(8,128)(2,1)} %do_hbm.1), custom_call_target="tpu_custom_call" | custom-call | tf_op jit(solution)/shard_map/pallas_call | solution.py:382
  120.4 0.0 copy-start.1
  120.4 2.8 %copy.11 = bf16[192,4096]{1,0:T(8,128)(2,1)} copy(bf16[192,4096]{1,0:T(8,128)(2,1)} %get-tuple-element.6) | data formatting | bytes 3145728
  123.2 0.0 copy-done.1
  123.2 0.0 copy-start
  123.2 0.9 copy.12
  124.1 0.5 copy-done
  124.6 0.9 copy.13
Async XLA Ops:
  120.4 2.8 %copy-start.1 = (bf16[192,2048]{1,0:T(8,128)(2,1)S(1)}, bf16[192,2048]{1,0:T(8,128)(2,1)}, u32[]{:S(2)}) copy-start(bf16[192,2048]{1,0:T(8,128)(2,1)} %get-tuple-element.7) | copy-start | bytes 2359300
  123.2 1.4 %copy-start = (bf16[192,2048]{1,0:T(8,128)(2,1)S(1)}, bf16[192,2048]{1,0:T(8,128)(2,1)}, u32[]{:S(2)}) copy-start(bf16[192,2048]{1,0:T(8,128)(2,1)} %get-tuple-element.8) | copy-start | bytes 2359300

commit v4 on v3

--- a/solution.py
+++ b/solution.py
@@ -163,7 +163,7 @@
 
     pl.semaphore_wait(barrier, heads + 1)
 
-    for first in (0, 2):
+    def send_all(first, lo, hi):
         def send(i, c):
             p = receiver(i)
 
@@ -174,7 +174,11 @@
 
             return c
 
-        lax.fori_loop(0, heads, send, 0)
+        lax.fori_loop(lo, hi, send, 0)
+
+    early = 10
+    send_all(0, 0, heads)
+    send_all(2, 0, early)
 
     def halo(i):
         ref = (kx, vx)[i]
@@ -197,6 +201,7 @@
         halo(0).start()
         halo(1).start()
 
+    send_all(2, early, heads)
     lax.fori_loop(0, late, kv_wait, 0)
 
     def turn(i, c):
@@ -301,8 +306,6 @@
             return c
 
         lax.fori_loop(0, per_quad, tile, 0)
-        deliver((0,), quad * 4, 4)
-
         @pl.when(n == at_stage(0, 1))
         def _():
             @pl.when(seq > 0)
@@ -310,6 +313,8 @@
                 stage(0, WINDOW)
                 rim(0).start()
                 rim(1).start()
+
+        deliver((0,), quad * 4, 4)
 
         for y, count in ((0, 4), (1, 4), (2, late - 8)):
             @pl.when(n == at_stage(y, min(2, quads - 1 - y)))

time: 126 us -> 119 us (0.944)
  the two profiles are of different devices: /device:TPU:1 before, /device:TPU:7 now
where the time goes in v4:
time: 119 us
  Pallas kernels  113 us (95%)
  local copies, waits for them, and re-layouts  5.07 us (4%)
    pallas_call x1, Pallas kernels, local(): pl.pallas_call(functools.partial(exchange_kernel, heads, groups), out_sha...  113 us
    unnamed x7, local copies, waits for them, and re-layouts  5.07 us

profile of v4, /device:TPU:7, one launch (start us, length us, event | category | flops | bytes accessed | tf_op | source)
XLA Modules:
  0.0 118.7 jit_solution(11973457345691012312)
XLA Ops:
  0.6 113.0 %shard_map.76 = (bf16[192,4096]{1,0:T(8,128)(2,1)}, bf16[192,2048]{1,0:T(8,128)(2,1)}, bf16[192,2048]{1,0:T(8,128)(2,1)}) custom-call(s32[16]{0:T(128)} %len_ref.1, bf16[192,4096]{1,0:T(8,128)(2,1)} %q_hbm.1, bf16[192,2048]{1,0:T(8,128)(2,1)} %k_hbm.1, bf16[192,2048]{1,0:T(8,128)(2,1)} %v_hbm.1, bf16[192,4096]{1,0:T(8,128)(2,1)} %do_hbm.1), custom_call_target="tpu_custom_call" | custom-call | tf_op jit(solution)/shard_map/pallas_call | solution.py:387
  113.6 0.0 copy-start.1
  113.6 2.8 %copy.11 = bf16[192,4096]{1,0:T(8,128)(2,1)} copy(bf16[192,4096]{1,0:T(8,128)(2,1)} %get-tuple-element.6) | data formatting | bytes 3145728
  116.4 0.0 copy-done.1
  116.4 0.0 copy-start
  116.4 0.9 copy.12
  117.3 0.5 copy-done
  117.8 0.9 copy.13
Async XLA Ops:
  113.6 2.8 %copy-start.1 = (bf16[192,2048]{1,0:T(8,128)(2,1)S(1)}, bf16[192,2048]{1,0:T(8,128)(2,1)}, u32[]{:S(2)}) copy-start(bf16[192,2048]{1,0:T(8,128)(2,1)} %get-tuple-element.7) | copy-start | bytes 2359300
  116.4 1.4 %copy-start = (bf16[192,2048]{1,0:T(8,128)(2,1)S(1)}, bf16[192,2048]{1,0:T(8,128)(2,1)}, u32[]{:S(2)}) copy-start(bf16[192,2048]{1,0:T(8,128)(2,1)} %get-tuple-element.8) | copy-start | bytes 2359300

commit v5 on v4

--- a/solution.py
+++ b/solution.py
@@ -93,14 +93,18 @@
     quads = heads // 4
     per_quad = tiles // quads
     mine, place = me // 4, lax.rem(me, 4)
-    start = lax.rem(mine + 1 + place, quads)
+
+    def turned(to):
+        return to // 2 + 2 * lax.rem(to, 2)
+
+    start = lax.rem(mine + 1 + turned(place), quads)
 
     def quad_at(n):
         return lax.rem(start + n, quads)
 
     def receiver(i):
         to = lax.rem(place + lax.rem(i, 4), 4)
-        return lax.rem(mine + 3 * quads - 1 - to - i // 4, quads) * 4 + to
+        return lax.rem(mine + 3 * quads - 1 - turned(to) - i // 4, quads) * 4 + to
 
     def peer(t):
         return lax.rem(me + t, heads)
@@ -153,6 +157,25 @@
     for kind in range(4):
         pltpu.make_async_copy(source(kind, me), target(kind, me), in_recv.at[kind, me]).start()
 
+    pl.semaphore_wait(barrier, heads + 1)
+
+    def send_all(first, lo, hi):
+        def send(i, c):
+            p = receiver(i)
+
+            @pl.when(p != me)
+            def _():
+                in_copy(first, p).start()
+                in_copy(first + 1, p).start()
+
+            return c
+
+        lax.fori_loop(lo, hi, send, 0)
+
+    early = 10
+    send_all(0, 0, heads)
+    send_all(2, 0, early)
+
     def clear(i, c):
         r = pl.multiple_of(i * BK, BK)
         dk[pl.ds(r, BK), :] = jnp.zeros((BK, HD), f32)
@@ -160,25 +183,6 @@
         return c
 
     lax.fori_loop(0, (WINDOW + group) // BK, clear, 0)
-
-    pl.semaphore_wait(barrier, heads + 1)
-
-    def send_all(first, lo, hi):
-        def send(i, c):
-            p = receiver(i)
-
-            @pl.when(p != me)
-            def _():
-                in_copy(first, p).start()
-                in_copy(first + 1, p).start()
-
-            return c
-
-        lax.fori_loop(lo, hi, send, 0)
-
-    early = 10
-    send_all(0, 0, heads)
-    send_all(2, 0, early)
 
     def halo(i):
         ref = (kx, vx)[i]
@@ -242,19 +246,20 @@
             device_id=(seq, j), device_id_type=MESH,
         )
 
+    def deliver_to(kinds, j):
+        for kind in kinds:
+            @pl.when(j != me)
+            def _():
+                out_copy(kind, j).start()
+
+            @pl.when(j == me)
+            def _():
+                src, dst = out_parts(kind, me)
+                pltpu.make_async_copy(src, dst, out_recv.at[kind, me]).start()
+
     def deliver(kinds, lo, count):
         def one(i, c):
-            j = lo + lax.rem(i + place, count)
-            for kind in kinds:
-                @pl.when(j != me)
-                def _():
-                    out_copy(kind, j).start()
-
-                @pl.when(j == me)
-                def _():
-                    src, dst = out_parts(kind, me)
-                    pltpu.make_async_copy(src, dst, out_recv.at[kind, me]).start()
-
+            deliver_to(kinds, lo + lax.rem(i + place, count))
             return c
 
         lax.fori_loop(0, count, one, 0)
@@ -279,6 +284,21 @@
         off = lax.rem(y - start + 2 * quads, quads)
         return jnp.where(off + over < quads, off + over, quads - 1)
 
+    def whole_at(y):
+        return at_stage(y, jnp.minimum(2, quads - 1 - y))
+
+    def in_turn(wanted):
+        def one(i, c):
+            j = quad_at(lax.rem(i, 4)) * 4 + lax.rem(place + i // 4 + lax.rem(i, 4), 4)
+
+            @pl.when(wanted(j))
+            def _():
+                deliver_to((1, 2), j)
+
+            return c
+
+        lax.fori_loop(0, heads, one, 0)
+
     def step(n, c):
         quad = quad_at(n)
 
@@ -317,14 +337,19 @@
         deliver((0,), quad * 4, 4)
 
         for y, count in ((0, 4), (1, 4), (2, late - 8)):
-            @pl.when(n == at_stage(y, min(2, quads - 1 - y)))
+            @pl.when(n == whole_at(y))
             def _():
                 stage(WINDOW + y * 4 * rows, count * rows)
-                deliver((1, 2), y * 4, count)
+
+                @pl.when(n < quads - 1)
+                def _():
+                    deliver((1, 2), y * 4, count)
 
         return c
 
     lax.fori_loop(0, quads, step, 0)
+
+    in_turn(lambda j: (j < late) & (whole_at(j // 4) == quads - 1))
 
     @pl.when(seq < groups - 1)
     def _():
@@ -344,7 +369,7 @@
 
     lax.fori_loop(0, WINDOW // 128, last, 0)
     stage(WINDOW + late * rows, (heads - late) * rows)
-    deliver((1, 2), late, heads - late)
+    in_turn(lambda j: j >= late)
 
     def finish(t, c):
         p = peer(t)

time: 119 us -> 118 us (level)
    pallas_call x1, Pallas kernels: 113 us -> 112 us  [local(): pl.pallas_call(functools.partial(exchange_kernel, heads, groups), out_sha...]
where the time goes in v5:
time: 118 us; the launch traced here: 117 us
  Pallas kernels  112 us (95%)
  local copies, waits for them, and re-layouts  5.07 us (4%)
    pallas_call x1, Pallas kernels, local(): pl.pallas_call(functools.partial(exchange_kernel, heads, groups), out_sha...  112 us
    unnamed x7, local copies, waits for them, and re-layouts  5.07 us

profile of v5, /device:TPU:7, one launch (start us, length us, event | category | flops | bytes accessed | tf_op | source)
XLA Modules:
  0.0 117.5 jit_solution(10632038482655281884)
XLA Ops:
  0.6 111.8 %shard_map.76 = (bf16[192,4096]{1,0:T(8,128)(2,1)}, bf16[192,2048]{1,0:T(8,128)(2,1)}, bf16[192,2048]{1,0:T(8,128)(2,1)}) custom-call(s32[16]{0:T(128)} %len_ref.1, bf16[192,4096]{1,0:T(8,128)(2,1)} %q_hbm.1, bf16[192,2048]{1,0:T(8,128)(2,1)} %k_hbm.1, bf16[192,2048]{1,0:T(8,128)(2,1)} %v_hbm.1, bf16[192,4096]{1,0:T(8,128)(2,1)} %do_hbm.1), custom_call_target="tpu_custom_call" | custom-call | tf_op jit(solution)/shard_map/pallas_call | solution.py:412
  112.4 0.0 copy-start.1
  112.4 2.8 %copy.11 = bf16[192,4096]{1,0:T(8,128)(2,1)} copy(bf16[192,4096]{1,0:T(8,128)(2,1)} %get-tuple-element.6) | data formatting | bytes 3145728
  115.2 0.0 copy-done.1
  115.2 0.0 copy-start
  115.2 0.9 copy.12
  116.1 0.5 copy-done
  116.6 0.9 copy.13
Async XLA Ops:
  112.4 2.8 %copy-start.1 = (bf16[192,2048]{1,0:T(8,128)(2,1)S(1)}, bf16[192,2048]{1,0:T(8,128)(2,1)}, u32[]{:S(2)}) copy-start(bf16[192,2048]{1,0:T(8,128)(2,1)} %get-tuple-element.7) | copy-start | bytes 2359300
  115.2 1.4 %copy-start = (bf16[192,2048]{1,0:T(8,128)(2,1)S(1)}, bf16[192,2048]{1,0:T(8,128)(2,1)}, u32[]{:S(2)}) copy-start(bf16[192,2048]{1,0:T(8,128)(2,1)} %get-tuple-element.8) | copy-start | bytes 2359300

commit v6 on v5

--- a/solution.py
+++ b/solution.py
@@ -33,6 +33,7 @@
     ki = lax.broadcasted_iota(jnp.int32,(BK,BQ),0)
     rows=[pl.ds(pl.multiple_of(b*BQ + t*BK, BK),BK) for t in range(NT)]
     stats=[]
+    ms=[]
     for h in range(per):
         q,do=qs[h],dos[h]
         m = None
@@ -45,7 +46,10 @@
             s_scr[h,t] = s
             mt = jnp.max(s.reshape(BK//8,8,BQ),axis=0)
             m = mt if m is None else jnp.maximum(m,mt)
-        m = jnp.max(m,axis=0,keepdims=True)
+        ms.append(jnp.max(m,axis=0,keepdims=True))
+    for h in range(per):
+        do = dos[h]
+        m = ms[h]
         l = jnp.zeros((8,BQ),f32); dd = jnp.zeros((8,BQ),f32)
         for t in range(NT):
             p = jnp.exp2((s_scr[h,t]-m)*C2)

time: 118 us -> 117 us (level)
  no operation moved by 1% of the time
where the time goes in v6:
time: 117 us
  Pallas kernels  111 us (95%)
  local copies, waits for them, and re-layouts  5.07 us (4%)
    pallas_call x1, Pallas kernels, local(): pl.pallas_call(functools.partial(exchange_kernel, heads, groups), out_sha...  111 us
    unnamed x7, local copies, waits for them, and re-layouts  5.07 us

profile of v6, /device:TPU:7, one launch (start us, length us, event | category | flops | bytes accessed | tf_op | source)
XLA Modules:
  0.0 116.7 jit_solution(8847484971443572740)
XLA Ops:
  0.6 111.0 %shard_map.76 = (bf16[192,4096]{1,0:T(8,128)(2,1)}, bf16[192,2048]{1,0:T(8,128)(2,1)}, bf16[192,2048]{1,0:T(8,128)(2,1)}) custom-call(s32[16]{0:T(128)} %len_ref.1, bf16[192,4096]{1,0:T(8,128)(2,1)} %q_hbm.1, bf16[192,2048]{1,0:T(8,128)(2,1)} %k_hbm.1, bf16[192,2048]{1,0:T(8,128)(2,1)} %v_hbm.1, bf16[192,4096]{1,0:T(8,128)(2,1)} %do_hbm.1), custom_call_target="tpu_custom_call" | custom-call | tf_op jit(solution)/shard_map/pallas_call | solution.py:416
  111.7 0.0 copy-start.1
  111.7 2.8 %copy.11 = bf16[192,4096]{1,0:T(8,128)(2,1)} copy(bf16[192,4096]{1,0:T(8,128)(2,1)} %get-tuple-element.6) | data formatting | bytes 3145728
  114.4 0.0 copy-done.1
  114.5 0.0 copy-start
  114.5 0.9 copy.12
  115.3 0.5 copy-done
  115.9 0.9 copy.13
Async XLA Ops:
  111.7 2.8 %copy-start.1 = (bf16[192,2048]{1,0:T(8,128)(2,1)S(1)}, bf16[192,2048]{1,0:T(8,128)(2,1)}, u32[]{:S(2)}) copy-start(bf16[192,2048]{1,0:T(8,128)(2,1)} %get-tuple-element.7) | copy-start | bytes 2359300
  114.5 1.4 %copy-start = (bf16[192,2048]{1,0:T(8,128)(2,1)S(1)}, bf16[192,2048]{1,0:T(8,128)(2,1)}, u32[]{:S(2)}) copy-start(bf16[192,2048]{1,0:T(8,128)(2,1)} %get-tuple-element.8) | copy-start | bytes 2359300

commit v7 on v6

--- a/solution.py
+++ b/solution.py
@@ -176,9 +176,19 @@
 
         lax.fori_loop(lo, hi, send, 0)
 
-    early = 10
-    send_all(0, 0, heads)
-    send_all(2, 0, early)
+    early = 8
+    late = (group - WINDOW) // rows
+
+    @pl.when(me >= late)
+    def _():
+        send_all(0, 0, heads)
+        send_all(2, 0, early)
+
+    @pl.when(me < late)
+    def _():
+        send_all(2, 0, 4)
+        send_all(0, 0, heads)
+        send_all(2, 4, early)
 
     def clear(i, c):
         r = pl.multiple_of(i * BK, BK)
@@ -201,7 +211,6 @@
         arrived(1, j)
         return c
 
-    late = (group - WINDOW) // rows
     lax.fori_loop(late, heads, kv_wait, 0)
 
     @pl.when(seq < groups - 1)

time: 117 us -> 115 us (0.983); the launches traced: 117 us -> 113 us
  Pallas kernels: 111 us -> 108 us
    pallas_call x1, Pallas kernels: 111 us -> 108 us  [local(): pl.pallas_call(functools.partial(exchange_kernel, heads, groups), out_sha...]
where the time goes in v7:
time: 115 us; the launch traced here: 113 us
  Pallas kernels  108 us (94%)
  local copies, waits for them, and re-layouts  5.07 us (4%)
    pallas_call x1, Pallas kernels, local(): pl.pallas_call(functools.partial(exchange_kernel, heads, groups), out_sha...  108 us
    unnamed x7, local copies, waits for them, and re-layouts  5.07 us

profile of v7, /device:TPU:7, one launch (start us, length us, event | category | flops | bytes accessed | tf_op | source)
XLA Modules:
  0.0 113.5 jit_solution(6442562236027950666)
XLA Ops:
  0.6 107.7 %shard_map.76 = (bf16[192,4096]{1,0:T(8,128)(2,1)}, bf16[192,2048]{1,0:T(8,128)(2,1)}, bf16[192,2048]{1,0:T(8,128)(2,1)}) custom-call(s32[16]{0:T(128)} %len_ref.1, bf16[192,4096]{1,0:T(8,128)(2,1)} %q_hbm.1, bf16[192,2048]{1,0:T(8,128)(2,1)} %k_hbm.1, bf16[192,2048]{1,0:T(8,128)(2,1)} %v_hbm.1, bf16[192,4096]{1,0:T(8,128)(2,1)} %do_hbm.1), custom_call_target="tpu_custom_call" | custom-call | tf_op jit(solution)/shard_map/pallas_call | solution.py:425
  108.4 0.0 copy-start.1
  108.4 2.8 %copy.11 = bf16[192,4096]{1,0:T(8,128)(2,1)} copy(bf16[192,4096]{1,0:T(8,128)(2,1)} %get-tuple-element.6) | data formatting | bytes 3145728
  111.2 0.0 copy-done.1
  111.2 0.0 copy-start
  111.2 0.9 copy.12
  112.0 0.5 copy-done
  112.6 0.9 copy.13
Async XLA Ops:
  108.4 2.8 %copy-start.1 = (bf16[192,2048]{1,0:T(8,128)(2,1)S(1)}, bf16[192,2048]{1,0:T(8,128)(2,1)}, u32[]{:S(2)}) copy-start(bf16[192,2048]{1,0:T(8,128)(2,1)} %get-tuple-element.7) | copy-start | bytes 2359300
  111.2 1.4 %copy-start = (bf16[192,2048]{1,0:T(8,128)(2,1)S(1)}, bf16[192,2048]{1,0:T(8,128)(2,1)}, u32[]{:S(2)}) copy-start(bf16[192,2048]{1,0:T(8,128)(2,1)} %get-tuple-element.8) | copy-start | bytes 2359300
